TPU v7x, 32 devices: a whole 2x2x4 slice. The times are simulated.
32 devices in a mesh: tile: 16 (over z, y, x), spec: 2 (over core).
Axes of the slice: x: 2, y: 2, z: 4, core: 2. Of those that a mesh axis runs over, the one named last changes fastest.
Arguments:
- tracers: float32 [48, 2, 2048, 128], P('spec', None, 'tile'), may hold values from 0.1 to 10
- courant: float32 [2, 2, 2, 2, 2048, 128], P('spec', None, None, None, 'tile'), may hold values from -0.4 to 0.4
- diffusivity: float32 [2, 2, 2, 2, 2048, 128], P('spec', None, None, None, 'tile'), may hold values from 0.005 to 0.08
- edge_blocks: int32 [16, 4], P('tile'), may hold values from 0 to 15, as said below
- edge_flips: int32 [16, 4], P('tile'), may hold values from 0 to 1, as said below
- roots: int32 [2, 16], P(None, 'tile'), may hold values from 0 to 1
Outputs:
- transported: float32 [48, 2, 2048, 128], P('spec', None, 'tile')
Inputs may be any that keep to these rules, and one draw needn't show every extreme that they name: `edge_blocks`: entries 0 to 3 of a row are the blocks across the west, east, south and north edges; if a is across b's east (north) edge then b is across a's west (south) edge; no block is across its own edge and the four blocks of a row differ. `edge_flips`: the flag of an edge equals the flag of the same edge seen from the block across it.
All inputs are finite; a program needn't handle non-finite values.
Results may differ from a plain program's by a relative error of at most 0.0003.
Values sent between devices are 32-bit elements; how exact they have to be, the bound alone decides.
A program may use at most 64 MiB of HBM per device.

v0:
```python
import jax
import jax.numpy as jnp
from jax import lax
from jax.sharding import PartitionSpec as P


def spread(x, axis, root):
    mine = lax.axis_index(axis) == root
    return lax.psum(jnp.where(mine, x, jnp.zeros_like(x)), axis)


def face_flux(padded, speed, kappa, along):
    inner = padded.shape[along] - 6

    def take_part(array, begin_at, end_at):
        return lax.slice_in_dim(array, begin_at, end_at, axis=along)

    edge_vals = 7.0 / 12.0 * (
        take_part(padded, 1, inner + 4) + take_part(padded, 2, inner + 5)
    ) - 1.0 / 12.0 * (take_part(padded, 0, inner + 3) + take_part(padded, 3, inner + 6))
    lower_face = take_part(edge_vals, 0, inner + 1)
    centre = take_part(edge_vals, 1, inner + 2)
    upper_face = take_part(edge_vals, 2, inner + 3)
    behind = take_part(padded, 2, inner + 3)
    ahead_cell = take_part(padded, 3, inner + 4)
    reverse = -speed
    shape_pos = 6.0 * behind - 3.0 * (lower_face + centre)
    from_behind = centre - 0.5 * speed * (
        centre - lower_face - (1.0 - 2.0 / 3.0 * speed) * shape_pos
    )
    shape_neg = 6.0 * ahead_cell - 3.0 * (centre + upper_face)
    from_ahead = centre + 0.5 * reverse * (
        upper_face - centre + (1.0 - 2.0 / 3.0 * reverse) * shape_neg
    )
    face_val = jnp.where(speed > 0.0, from_behind, from_ahead)
    return speed * face_val - kappa * (ahead_cell - behind)


def edge_strips(field):
    west_side = jnp.swapaxes(field[..., :, 0:3], -1, -2)
    east_side = jnp.swapaxes(field[..., :, ::-1][..., :, 0:3], -1, -2)
    south_side = field[..., 0:3, :]
    north_side = field[..., ::-1, :][..., 0:3, :]
    return jnp.stack([west_side, east_side, south_side, north_side], 0)


def orient(strip_in, flipped):
    return jnp.where(flipped == 1, strip_in[..., ::-1], strip_in)


def advance(
    field,
    speed_x,
    speed_y,
    kappa_x,
    kappa_y,
    from_west,
    from_east,
    from_south,
    from_north,
    east_speed,
    east_kappa,
    north_speed,
    north_kappa,
):
    padded_x = jnp.concatenate(
        [jnp.swapaxes(from_west[..., ::-1, :], -1, -2), field, jnp.swapaxes(from_east, -1, -2)], -1
    )
    padded_y = jnp.concatenate([from_south[..., ::-1, :], field, from_north], -2)
    faces_cx = jnp.concatenate([speed_x, east_speed[..., None]], -1)
    faces_kx = jnp.concatenate([kappa_x, east_kappa[..., None]], -1)
    faces_cy = jnp.concatenate([speed_y, north_speed[..., None, :]], -2)
    faces_ky = jnp.concatenate([kappa_y, north_kappa[..., None, :]], -2)
    flux_x = face_flux(padded_x, faces_cx, faces_kx, padded_x.ndim - 1)
    flux_y = face_flux(padded_y, faces_cy, faces_ky, padded_y.ndim - 2)
    return field - (flux_x[..., 1:] - flux_x[..., :-1]) - (flux_y[..., 1:, :] - flux_y[..., :-1, :])


def local_substep(field, speeds, kappas, neighbours, flips):
    strips = edge_strips(field)
    west_faces = jnp.stack([speeds[0][..., :, 0], kappas[0][..., :, 0]])
    south_faces = jnp.stack([speeds[1][..., 0, :], kappas[1][..., 0, :]])
    faces = jnp.stack([west_faces, south_faces])
    every_strip, every_face = (
        lax.all_gather(strips[None], "tile", axis=0, tiled=True),
        lax.all_gather(faces[None], "tile", axis=0, tiled=True),
    )
    from_west = every_strip[neighbours[0], 1]
    from_east = every_strip[neighbours[1], 0]
    from_south = every_strip[neighbours[2], 3]
    from_north = every_strip[neighbours[3], 2]
    east_faces = every_face[neighbours[1], 0]
    north_faces = every_face[neighbours[3], 1]
    from_west = orient(from_west, flips[0])
    from_east = orient(from_east, flips[1])
    from_south = orient(from_south, flips[2])
    from_north = orient(from_north, flips[3])
    east_faces = orient(east_faces, flips[1])
    north_faces = orient(north_faces, flips[3])
    return advance(
        field,
        speeds[0],
        speeds[1],
        kappas[0],
        kappas[1],
        from_west,
        from_east,
        from_south,
        from_north,
        east_faces[0],
        east_faces[1],
        north_faces[0],
        north_faces[1],
    )


def body(tracers, courant, diffusivity, edge_blocks, edge_flips, roots):
    neighbours = edge_blocks[0]
    flips = edge_flips[0]
    field = tracers
    for substep in range(courant.shape[1]):
        speeds, kappas = (
            spread(courant[0, substep], "spec", roots[substep, 0]),
            spread(diffusivity[0, substep], "spec", roots[substep, 0]),
        )
        field = local_substep(field, speeds, kappas, neighbours, flips)
    return field


def solution(mesh):
    placed = (
        P("spec", None, "tile", None),
        P("spec", None, None, None, "tile", None),
        P("spec", None, None, None, "tile", None),
        P("tile", None),
        P("tile", None),
        P(None, "tile"),
    )
    return jax.shard_map(
        body, mesh=mesh, in_specs=placed, out_specs=P("spec", None, "tile", None), check_vma=False
    )
```

profile of v0, /device:TPU:0, one launch (start us, length us, event | category | flops | bytes accessed | tf_op | source)
XLA Modules:
  0.0 382.2 jit_solution(13666697230982655151)
XLA Ops:
  15.9 3.9 %copy.310 = f32[24,2,128,128]{3,0,2,1:T(8,128)S(1)} copy(f32[24,2,128,128]{3,2,1,0:T(8,128)} %param.6) | data formatting | bytes 6291456 | tf_op args[0]
  19.8 3.9 %fusion.38 = (f32[24,2,128,3]{3,2,1,0:T(8,128)}, f32[24,2,128,3]{3,2,1,0:T(8,128)}) fusion(f32[24,2,128,128]{3,2,1,0:T(8,128)S(1)} %copy-done), kind=kLoop, calls=%fused_computation.164 | loop fusion | bytes 294912 | tf_op jit(solution)/shard_map/slice | solution.py:40
  23.7 2.7 copy.349
  26.4 2.4 copy.348
  50.4 43.1 %all-gather.2 = f32[32,2,2,128]{3,2,1,0:T(2,128)S(1)} all-gather(f32[2,2,2,128]{3,2,1,0:T(2,128)S(1)} %pad_maximum_fusion.23), channel_id=4, replica_groups=mesh['tile'=16,'spec'=2] {'tile'}, dimensions={0}, use_global_device_ids=true | all-gather | bytes 69632 | tf_op jit(solution)/shard_map/all_gather | solution.py:86
  94.8 36.2 %all-gather = f32[32,2,2,128]{3,2,1,0:T(2,128)S(1)} all-gather(f32[2,2,2,128]{3,2,1,0:T(2,128)S(1)} %pad_maximum_fusion.22), channel_id=2, replica_groups=mesh['tile'=16,'spec'=2] {'tile'}, dimensions={0}, use_global_device_ids=true | all-gather | bytes 69632 | tf_op jit(solution)/shard_map/all_gather | solution.py:86
  152.1 3.1 copy.300
  155.2 4.9 %fusion.24 = f32[24,2,128,3]{3,0,2,1:T(8,128)} fusion(f32[24,2,3,128]{2,0,3,1:T(8,128)} %bitcast.137, pred[]{:T(512)} %bitcast.3), kind=kLoop, calls=%fused_computation.60 | loop fusion | flops 18432 | bytes 147457 | tf_op jit(solution)/shard_map/transpose | solution.py:67
  160.1 2.9 copy.299
  163.0 4.8 %reverse_select_fusion.3 = f32[24,2,3,128]{2,0,3,1:T(8,128)} fusion(f32[24,2,3,128]{2,0,3,1:T(8,128)} %bitcast.138, pred[]{:T(512)} %bitcast.18), kind=kLoop, calls=%fused_computation.33 | loop fusion | flops 18432 | bytes 147457 | tf_op jit(solution)/shard_map/jit(_where)/select_n | solution.py:48
  167.8 6.1 %rev.54 = f32[24,2,3,128]{2,0,3,1:T(8,128)} reverse(f32[24,2,3,128]{2,0,3,1:T(8,128)} %reverse_select_fusion.3), dimensions={2} | reverse | bytes 147456 | tf_op jit(solution)/shard_map/rev | solution.py:67
  173.8 5.5 %pad_maximum_fusion.4 = f32[24,2,128,134]{3,0,2,1:T(8,128)S(1)} fusion(f32[24,2,128,3]{3,0,2,1:T(8,128)} %fusion.24, f32[24,2,128,128]{3,0,2,1:T(8,128)S(1)} %copy.310, f32[24,2,128,3]{3,0,2,1:T(8,128)} %bitcast.132), kind=kLoop, calls=%fused_computation.26 | loop fusion | flops 1646592 | bytes 6586368 | tf_op jit(solution)/shard_map/concatenate | solution.py:66
  179.3 6.7 %fusion.8 = f32[24,2,128,131]{3,0,2,1:T(8,128)} fusion(f32[24,2,128,3]{3,0,2,1:T(8,128)S(1)} %copy-done.2, f32[24,2,128,128]{3,0,2,1:T(8,128)S(1)} %copy.310, f32[24,2,128,3]{3,0,2,1:T(8,128)S(1)} %bitcast.133, f32[24,2,128,134]{3,0,2,1:T(8,128)S(1)} %pad_maximum_fusion.4), kind=kLoop, calls=%fused_computation.20 | loop fusion | flops 5634048 | bytes 12951552 | tf_op jit(solution)/shard_map/sub | solution.py:18
  196.8 12.0 %multiply_subtract_fusion.1 = f32[24,2,128,129]{3,0,2,1:T(8,128)} fusion(f32[24,2,128,3]{3,0,2,1:T(8,128)S(1)} %copy-done.3, f32[24,2,128,128]{3,0,2,1:T(8,128)S(1)} %copy.310, f32[24,2,128,131]{3,0,2,1:T(8,128)S(1)} %bitcast.126, f32[24,2,128,3]{3,0,2,1:T(8,128)S(1)} %bitcast.134, f32[2,128,129]{2,1,0:T(8,128)S(1)} %copy-done.17, ...), kind=kLoop, calls=%fused_computation.29 | loop fusion | flops 19814400 | bytes 16800000 | tf_op jit(solution)/shard_map/sub | solution.py:36
  208.8 5.9 %multiply_subtract_fusion.3 = f32[24,2,129,128]{3,0,2,1:T(8,128)S(1)} fusion(f32[24,2,3,128]{3,0,2,1:T(8,128)S(1)} %get-tuple-element.81, f32[24,2,131,128]{3,0,2,1:T(8,128)S(1)} %fusion.17, f32[24,2,3,128]{3,0,2,1:T(8,128)S(1)} %copy-done.10, f32[24,2,128,128]{3,0,2,1:T(8,128)S(1)} %copy.310, f32[2,129,128]{2,1,0:T(8,128)S(1)} %copy-done.24, ...), kind=kLoop, calls=%fused_computation.59 | loop fusion | flops 19814400 | bytes 16800000 | tf_op jit(solution)/shard_map/sub | solution.py:36
  214.7 6.3 %fusion.28 = f32[24,2,128,128]{3,0,2,1:T(8,128)S(1)} fusion(f32[24,2,129,128]{3,0,2,1:T(8,128)S(1)} %multiply_subtract_fusion.3, f32[24,2,128,129]{3,0,2,1:T(8,128)} %multiply_subtract_fusion.1, f32[24,2,128,128]{3,2,1,0:T(8,128)S(1)} %copy-done.1), kind=kLoop, calls=%fused_computation.68 | loop fusion | flops 3145728 | bytes 18874368 | tf_op jit(solution)/shard_map/sub | solution.py:76
  221.0 3.7 slice_bitcast_fusion
  225.4 6.1 %slice.377 = f32[24,2,128,3]{3,0,2,1:T(8,128)} reverse(f32[24,2,128,3]{3,0,2,1:T(8,128)} %get-tuple-element.18), dimensions={3} | reverse | bytes 147456 | tf_op jit(solution)/shard_map/slice | solution.py:41
  231.4 2.4 copy.329
  233.8 3.0 copy.328
  252.5 64.6 %all-gather.9.cloned.1.call-done = f32[64,24,2,3,128]{4,1,3,2,0:T(8,128)} async-done(((f32[4,24,2,3,128]{4,1,3,2,0:T(8,128)}), f32[64,24,2,3,128]{4,1,3,2,0:T(8,128)}) %all-gather.9.cloned.1.call-update) | async-done | bytes 4718608 | tf_op jit(solution)/shard_map/all_gather | solution.py:85
  318.1 2.2 copy.353
  320.3 4.8 %reverse_select_fusion.1 = f32[24,2,3,128]{2,0,3,1:T(8,128)} fusion(f32[24,2,3,128]{2,0,3,1:T(8,128)} %bitcast.135, pred[]{:T(512)} %bitcast.18), kind=kLoop, calls=%fused_computation.31 | loop fusion | flops 18432 | bytes 147457 | tf_op jit(solution)/shard_map/jit(_where)/select_n | solution.py:48
  325.1 6.0 %rev.62 = f32[24,2,3,128]{2,0,3,1:T(8,128)} reverse(f32[24,2,3,128]{2,0,3,1:T(8,128)} %reverse_select_fusion.1), dimensions={2} | reverse | bytes 147456 | tf_op jit(solution)/shard_map/rev | solution.py:67
  331.1 2.2 copy.354
  333.3 3.3 fusion.25
  337.1 2.5 pad_maximum_fusion.5
  339.6 7.0 %fusion.3 = f32[24,2,128,131]{3,0,2,1:T(8,128)} fusion(f32[24,2,128,3]{3,0,2,1:T(8,128)S(1)} %fusion.25, f32[24,2,128,128]{3,0,2,1:T(8,128)S(1)} %fusion.28, f32[24,2,128,3]{3,0,2,1:T(8,128)S(1)} %bitcast.130, f32[24,2,128,134]{3,0,2,1:T(8,128)S(1)} %pad_maximum_fusion.5), kind=kLoop, calls=%fused_computation.15 | loop fusion | flops 5634048 | bytes 12951552 | tf_op jit(solution)/shard_map/sub | solution.py:18
  351.5 8.9 %multiply_subtract_fusion = f32[24,2,128,129]{3,0,2,1:T(8,128)S(1)} fusion(f32[24,2,128,3]{3,0,2,1:T(8,128)S(1)} %copy-done.7, f32[24,2,128,128]{3,0,2,1:T(8,128)S(1)} %fusion.28, f32[24,2,128,131]{3,0,2,1:T(8,128)S(1)} %bitcast.128, f32[24,2,128,3]{3,0,2,1:T(8,128)S(1)} %bitcast.131, f32[2,128,129]{2,1,0:T(8,128)} %copy.336, f32[2,128,129]{2,1,0:T(8,128)} %copy.335, ...), kind=kLoop, calls=%fused_computation.28 | loop fusion | flops 19814400 | bytes 16800000 | tf_op jit(solution)/shard_map/sub | solution.py:36
  360.4 7.0 %multiply_subtract_fusion.2 = f32[24,2,129,128]{3,0,2,1:T(8,128)S(1)} fusion(f32[24,2,3,128]{3,0,2,1:T(8,128)S(1)} %broadcast_select_fusion, f32[24,2,131,128]{3,0,2,1:T(8,128)S(1)} %fusion.14, f32[24,2,3,128]{3,0,2,1:T(8,128)S(1)} %rev.66, f32[24,2,128,128]{3,0,2,1:T(8,128)S(1)} %fusion.28, f32[2,129,128]{2,1,0:T(8,128)} %copy.343, ...), kind=kLoop, calls=%fused_computation.58 | loop fusion | flops 19814400 | bytes 16800000 | tf_op jit(solution)/shard_map/sub | solution.py:36
  367.4 2.8 fusion.26
  370.2 4.2 %copy.344 = f32[24,2,128,128]{3,2,1,0:T(8,128)} copy(f32[24,2,128,128]{3,0,2,1:T(8,128)} %fusion.26) | data formatting | bytes 6291456 | tf_op jit(solution)/shard_map/sub | solution.py:76
  (184 shorter events, 74.3 us)
Async XLA Ops:
  7.4 33.8 %all-reduce.3.cloned.1.call-start = ((), (), s32[]{:S(2)}) async-start(), calls=%async_computation.2 | async-start | bytes 2097152 | tf_op jit(solution)/shard_map/psum | solution.py:9
  15.9 134.5 %all-gather.7.cloned.1.call-start = ((), (), s32[]{:S(2)}) async-start(), calls=%async_computation | async-start | bytes 5013504 | tf_op jit(solution)/shard_map/all_gather | solution.py:85
  15.9 3.9 %copy-start = (f32[24,2,128,128]{3,2,1,0:T(8,128)S(1)}, f32[24,2,128,128]{3,2,1,0:T(8,128)}, u32[]{:S(2)}) copy-start(f32[24,2,128,128]{3,2,1,0:T(8,128)} %param.6) | copy-start | bytes 9437188
  23.7 6.0 %copy-start.28 = (s32[1,4]{1,0:T(1,128)S(1)}, s32[1,4]{1,0:T(1,128)}, u32[]{:S(2)}) copy-start(s32[1,4]{1,0:T(1,128)} %param.9) | copy-start | bytes 52
  23.7 11.7 %copy-start.29 = (s32[1,4]{1,0:T(1,128)S(1)}, s32[1,4]{1,0:T(1,128)}, u32[]{:S(2)}) copy-start(s32[1,4]{1,0:T(1,128)} %param.10) | copy-start | bytes 52
  29.7 287.4 %all-gather.9.cloned.1.call-start = ((), (), s32[]{:S(2)}) async-start(), calls=%async_computation.1 | async-start | bytes 5013504 | tf_op jit(solution)/shard_map/all_gather | solution.py:85
  152.1 35.5 %copy-start.18 = (f32[24,2,3,128]{3,0,2,1:T(8,128)}, f32[24,2,3,128]{3,0,2,1:T(8,128)S(1)}, u32[]{:S(2)}) copy-start(f32[24,2,3,128]{3,0,2,1:T(8,128)S(1)} %get-tuple-element.14) | copy-start | bytes 221188
  173.8 5.5 %copy-start.2 = (f32[24,2,128,3]{3,0,2,1:T(8,128)S(1)}, f32[24,2,128,3]{3,0,2,1:T(8,128)}, u32[]{:S(2)}) copy-start(f32[24,2,128,3]{3,0,2,1:T(8,128)} %fusion.24) | copy-start | bytes 221188
  173.8 5.5 %copy-start.8 = (f32[24,2,3,128]{2,0,3,1:T(8,128)S(1)}, f32[24,2,3,128]{2,0,3,1:T(8,128)}, u32[]{:S(2)}) copy-start(f32[24,2,3,128]{2,0,3,1:T(8,128)} %rev.54) | copy-start | bytes 221188
  192.7 2.8 copy-start.3
  192.7 3.7 copy-start.9
  192.8 3.7 copy-start.12
  192.8 3.7 copy-start.13
  192.8 3.7 copy-start.14
  192.8 3.8 copy-start.15
  192.8 3.9 %copy-start.16 = (f32[2,128,129]{2,1,0:T(8,128)S(1)}, f32[2,128,129]{2,1,0:T(8,128)}, u32[]{:S(2)}) copy-start(f32[2,128,129]{2,1,0:T(8,128)} %copy.307) | copy-start | bytes 396292
  192.8 3.9 %copy-start.17 = (f32[2,128,129]{2,1,0:T(8,128)S(1)}, f32[2,128,129]{2,1,0:T(8,128)}, u32[]{:S(2)}) copy-start(f32[2,128,129]{2,1,0:T(8,128)} %copy.309) | copy-start | bytes 396292
  192.8 3.9 %copy-start.27 = (pred[2,128,129]{2,1,0:T(8,128)(4,1)S(1)}, pred[2,128,129]{2,1,0:T(8,128)(4,1)}, u32[]{:S(2)}) copy-start(pred[2,128,129]{2,1,0:T(8,128)(4,1)} %copy.294) | copy-start | bytes 99076
  196.7 12.1 %copy-start.19 = (f32[2,129,128]{2,1,0:T(8,128)S(1)}, f32[2,129,128]{2,1,0:T(8,128)}, u32[]{:S(2)}) copy-start(f32[2,129,128]{2,1,0:T(8,128)} %copy.311) | copy-start | bytes 396292
  196.7 12.1 %copy-start.20 = (f32[2,129,128]{2,1,0:T(8,128)S(1)}, f32[2,129,128]{2,1,0:T(8,128)}, u32[]{:S(2)}) copy-start(f32[2,129,128]{2,1,0:T(8,128)} %copy.316) | copy-start | bytes 396292
  196.7 12.1 %copy-start.21 = (f32[2,129,128]{2,1,0:T(8,128)S(1)}, f32[2,129,128]{2,1,0:T(8,128)}, u32[]{:S(2)}) copy-start(f32[2,129,128]{2,1,0:T(8,128)} %copy.317) | copy-start | bytes 396292
  196.7 12.1 %copy-start.22 = (f32[2,129,128]{2,1,0:T(8,128)S(1)}, f32[2,129,128]{2,1,0:T(8,128)}, u32[]{:S(2)}) copy-start(f32[2,129,128]{2,1,0:T(8,128)} %copy.318) | copy-start | bytes 396292
  196.7 12.1 %copy-start.23 = (f32[2,129,128]{2,1,0:T(8,128)S(1)}, f32[2,129,128]{2,1,0:T(8,128)}, u32[]{:S(2)}) copy-start(f32[2,129,128]{2,1,0:T(8,128)} %copy.319) | copy-start | bytes 396292
  196.8 12.1 %copy-start.24 = (f32[2,129,128]{2,1,0:T(8,128)S(1)}, f32[2,129,128]{2,1,0:T(8,128)}, u32[]{:S(2)}) copy-start(f32[2,129,128]{2,1,0:T(8,128)} %copy.320) | copy-start | bytes 396292
  208.8 5.9 %copy-start.1 = (f32[24,2,128,128]{3,2,1,0:T(8,128)S(1)}, f32[24,2,128,128]{3,2,1,0:T(8,128)}, u32[]{:S(2)}) copy-start(f32[24,2,128,128]{3,2,1,0:T(8,128)} %param.6) | copy-start | bytes 9437188
  239.6 4.1 %copy-start.25 = (f32[1,2,128,128]{2,1,3,0:T(2,128)S(1)}, f32[1,2,128,128]{2,1,3,0:T(2,128)}, u32[]{:S(2)}) copy-start(f32[1,2,128,128]{2,1,3,0:T(2,128)} %copy.352) | copy-start | bytes 393220
  333.3 3.7 copy-start.4
  336.6 2.9 copy-start.6
  347.0 3.6 copy-start.5
  347.0 4.5 %copy-start.7 = (f32[24,2,128,3]{3,0,2,1:T(8,128)S(1)}, f32[24,2,128,3]{3,0,2,1:T(8,128)}, u32[]{:S(2)}) copy-start(f32[24,2,128,3]{3,0,2,1:T(8,128)} %copy-done.6) | copy-start | bytes 221188
  347.0 4.5 %copy-start.11 = (f32[2,128,129]{2,1,0:T(8,128)S(1)}, f32[2,128,129]{2,1,0:T(8,128)}, u32[]{:S(2)}) copy-start(f32[2,128,129]{2,1,0:T(8,128)} %copy.326) | copy-start | bytes 396292
  347.0 4.5 %copy-start.26 = (pred[2,128,129]{2,1,0:T(8,128)(4,1)S(1)}, pred[2,128,129]{2,1,0:T(8,128)(4,1)}, u32[]{:S(2)}) copy-start(pred[2,128,129]{2,1,0:T(8,128)(4,1)} %copy.327) | copy-start | bytes 99076
  (5 other events, 10.4 us)
Sparse Core Ops, SparseCore 0:
  16.0 22.3 all-reduce.2
Sparse Core Ops, SparseCore 1:
  29.8 83.9 all-gather.6
  239.4 77.6 all-gather.8
where the time goes:
time: 390 us; the launch traced here: 382 us
  local copies, waits for them, and re-layouts  108 us (28%)
  other arithmetic  103 us (26%)
  blocking collectives  79.3 us (20%)
  waiting for transfers between devices  64.6 us (17%)
  between operations  27.2 us (7%)
    all_gather x2, blocking collectives, local_substep(): lax.all_gather(faces[None], 'tile', axis=0, tiled=True)  79.3 us
    all_gather x2, waiting for transfers between devices, local_substep(): lax.all_gather(strips[None], 'tile', axis=0, tiled=True)  64.6 us
    sub x4, other arithmetic, face_flux(): return speed * face_val - kappa * (ahead_cell - behind)  33.8 us
    unnamed x75, local copies, waits for them, and re-layouts  21.1 us
    sub x4, other arithmetic, face_flux(): 7.0 / 12.0  15.6 us
    rev x2, local copies, waits for them, and re-layouts, advance(): from_west[..., ::-1, :]  12.1 us
    select_n x9, other arithmetic, orient(): return jnp.where(flipped == 1, strip_in[..., ::-1], strip_in)  11.2 us
    another operation x8, local copies, waits for them, and re-layouts, edge_strips(): return jnp.stack([west_side, east_side, south_side, north_side], 0)  10.6 us
  transfers between devices with their start and end apart: 3, of which 1 were waited for; matrix products, arithmetic and copies ran while one was open for 15% of the time, Pallas kernels for 0%

commit v1 on v0

v1 whole, which is shorter than its diff:
```python
import functools

import jax
import jax.numpy as jnp
from jax import lax
from jax.experimental import pallas as pl
from jax.experimental.pallas import tpu as pltpu
from jax.sharding import PartitionSpec as P

MESH = pl.DeviceIdType.MESH
C = 128
PAD = 144
VMEM_LIMIT = 56 * 1024 * 1024


def greet_all(sizes, axis):
    n = sizes[axis]
    me = lax.axis_index(axis)
    barrier = pltpu.get_barrier_semaphore()

    @pl.loop(1, n)
    def _(off):
        pl.semaphore_signal(
            barrier, inc=1, device_id={axis: lax.rem(me + off, n)}, device_id_type=MESH
        )

    pl.semaphore_wait(barrier, n - 1)


def spread_kernel(sizes, cour, diff, cour_all, diff_all, send_sem, recv_sem, own_sem):
    n = sizes["spec"]
    me = lax.axis_index("spec")
    greet_all(sizes, "spec")
    own = [
        pltpu.make_async_copy(cour.at[0], cour_all.at[me], own_sem.at[0]),
        pltpu.make_async_copy(diff.at[0], diff_all.at[me], own_sem.at[1]),
    ]

    def copies(off):
        peer = lax.rem(me + off, n)
        return [
            pltpu.make_async_remote_copy(
                src_ref=src.at[0],
                dst_ref=dst.at[me],
                send_sem=send_sem.at[which, off],
                recv_sem=recv_sem.at[which, off],
                device_id={"spec": peer},
                device_id_type=MESH,
            )
            for which, (src, dst) in enumerate([(cour, cour_all), (diff, diff_all)])
        ]

    @pl.loop(1, n)
    def _(off):
        for copy in copies(off):
            copy.start()

    for copy in own:
        copy.start()
    for copy in own:
        copy.wait()

    @pl.loop(1, n)
    def _(off):
        for copy in copies(off):
            copy.wait()


def swap_kernel(sizes, slots, got, send_sem, recv_sem):
    n = sizes["tile"]
    me = lax.axis_index("tile")
    greet_all(sizes, "tile")

    def copy_to(off):
        peer = lax.rem(me + off, n)
        return pltpu.make_async_remote_copy(
            src_ref=slots.at[peer],
            dst_ref=got.at[me],
            send_sem=send_sem.at[off],
            recv_sem=recv_sem.at[off],
            device_id={"tile": peer},
            device_id_type=MESH,
        )

    @pl.loop(1, n)
    def _(off):
        copy_to(off).start()

    @pl.loop(1, n)
    def _(off):
        copy_to(off).wait()


def spread_fields(sizes, cour, diff):
    n = sizes["spec"]
    shape = jax.ShapeDtypeStruct((n,) + cour.shape[1:], cour.dtype)
    anywhere = pl.BlockSpec(memory_space=pl.ANY)
    return pl.pallas_call(
        functools.partial(spread_kernel, sizes),
        out_shape=(shape, shape),
        in_specs=[anywhere] * 2,
        out_specs=(anywhere, anywhere),
        scratch_shapes=[
            pltpu.SemaphoreType.DMA((2, n)),
            pltpu.SemaphoreType.DMA((2, n)),
            pltpu.SemaphoreType.DMA((2,)),
        ],
        compiler_params=pltpu.CompilerParams(collective_id=0, has_side_effects=True),
        name="spread_fields",
    )(cour, diff)


def swap_slots(sizes, slots, which):
    n = sizes["tile"]
    anywhere = pl.BlockSpec(memory_space=pl.ANY)
    return pl.pallas_call(
        functools.partial(swap_kernel, sizes),
        out_shape=jax.ShapeDtypeStruct(slots.shape, slots.dtype),
        in_specs=[anywhere],
        out_specs=anywhere,
        scratch_shapes=[pltpu.SemaphoreType.DMA((n,)), pltpu.SemaphoreType.DMA((n,))],
        compiler_params=pltpu.CompilerParams(collective_id=1 + which, has_side_effects=True),
        name=f"swap_slots_{which}",
    )(slots)


def groups_of(planes):
    return -(-planes // 16)


def lanes(rows):
    return lax.broadcasted_iota(jnp.int32, (rows, C), 1)


def pack_strips(planes, q, strips, turned):
    lane_group = lanes(C) // 8
    for g in range(groups_of(planes)):
        packed = jnp.zeros((C, C), jnp.float32)
        for slot in range(min(16, planes - 16 * g)):
            plane = q[pl.ds((16 * g + slot) * C, C), :]
            packed = jnp.where(lane_group == slot, pltpu.roll(plane, 8 * slot + 3, 1), packed)
        turned[pl.ds(g * C, C), :] = packed.T
    for d in range(3):
        rows = pl.ds(d * planes, planes)
        strips[0, rows, :] = turned[pl.ds(3 + d, planes, stride=8), :]
        strips[1, rows, :] = turned[pl.ds(2 - d, planes, stride=8), :]
        strips[2, rows, :] = q[pl.ds(d, planes, stride=C), :]
        strips[3, rows, :] = q[pl.ds(C - 1 - d, planes, stride=C), :]


def fill_slots(n, near, strips, slots):
    @pl.loop(0, n)
    def _(dest):
        edge = jnp.int32(0)
        for e in range(1, 4):
            edge = jnp.where(near[0, e] == dest, e, edge)
        slots[dest] = strips[edge]


def pack_kernel(sizes, planes, roots, near, q, cour0, cour1, diff0, diff1, slots, strips, turned):
    pack_strips(planes, q, strips, turned)
    lane = lanes(C)
    faces = jnp.zeros((C, C), jnp.float32)
    for k, fields in enumerate([(cour0, diff0), (cour1, diff1)]):
        for t, field in enumerate(fields):
            for lev in range(2):
                j = (k * 2 + t) * 2 + lev
                west = field[0, 0, 0, lev]
                west = pltpu.roll(west, j, 1) if j else west
                faces = jnp.where(lane == j, west, faces)
                strips[2, pl.ds(3 * planes + j, 1), :] = field[0, 0, 1, lev, 0:1, :]
    strips[0, pl.ds(3 * planes, 8), :] = faces.T[0:8]
    strips[1, pl.ds(3 * planes, 8), :] = jnp.zeros((8, C), jnp.float32)
    strips[3, pl.ds(3 * planes, 8), :] = jnp.zeros((8, C), jnp.float32)
    fill_slots(sizes["tile"], near, strips, slots)


def field_spec(k):
    return pl.BlockSpec(
        (1, 1, 2, 2, C, C), lambda i, roots, *_: (roots[k, 0], k, 0, 0, 0, 0)
    )


def whole_spec(shape):
    return pl.BlockSpec(shape, lambda i, *_: (0,) * len(shape))


def pack_first(sizes, roots, near, q, cour_all, diff_all):
    planes = q.shape[0] // C
    n = sizes["tile"]
    rows = 3 * planes + 8
    return pl.pallas_call(
        functools.partial(pack_kernel, sizes, planes),
        out_shape=jax.ShapeDtypeStruct((n, rows, C), jnp.float32),
        grid_spec=pltpu.PrefetchScalarGridSpec(
            num_scalar_prefetch=2,
            grid=(1,),
            in_specs=[
                whole_spec(q.shape),
                field_spec(0),
                field_spec(1),
                field_spec(0),
                field_spec(1),
            ],
            out_specs=whole_spec((n, rows, C)),
            scratch_shapes=[
                pltpu.VMEM((4, rows, C), jnp.float32),
                pltpu.VMEM((groups_of(planes) * C, C), jnp.float32),
            ],
        ),
        compiler_params=pltpu.CompilerParams(vmem_limit_bytes=VMEM_LIMIT),
        name="pack_first",
    )(roots, near, q, cour_all, cour_all, diff_all, diff_all)


def orientation(flipped):
    row = lax.broadcasted_iota(jnp.int32, (C, C), 0)
    col = lax.broadcasted_iota(jnp.int32, (C, C), 1)
    target = jnp.where(flipped == 1, C - 1 - row, row)
    return jnp.where(col == target, 1.0, 0.0).astype(jnp.float32)


def oriented(rows, turn):
    return jnp.dot(
        rows, turn, precision=lax.Precision.HIGHEST, preferred_element_type=jnp.float32
    )


def taps(c, k):
    s = jnp.abs(c)
    rest = 1.0 - s
    mid = c * rest * rest
    outer = -s * rest
    ahead = (3.0 - 2.0 * s) * s
    pos = jnp.maximum(c, 0.0)
    neg = jnp.minimum(c, 0.0)
    out_pos = pos * outer
    out_neg = neg * outer
    a = 7.0 / 12.0
    b = -1.0 / 12.0
    return [
        b * out_pos,
        b * mid + a * out_pos,
        a * (mid + out_pos) + b * out_neg + pos * ahead + k,
        a * (mid + out_neg) + b * out_pos + neg * ahead - k,
        b * mid + a * out_neg,
        b * out_neg,
    ]


def stencil(low, high):
    zero = [None]
    lo = low + zero
    hi = zero + high
    result = []
    for a, b in zip(lo, hi):
        result.append(-b if a is None else a if b is None else a - b)
    return result


def step_kernel(
    sizes, planes, k, last, roots, near, flips, q, cour, diff, got_faces, got, *rest
):
    if last:
        out, padded, turned, ghosts, coef, south, faces = rest
    else:
        out, slots, padded, turned, ghosts, coef, south, faces, strips = rest
    groups = groups_of(planes)

    @pl.loop(0, planes)
    def _(p):
        padded[pl.ds(pl.multiple_of(p * PAD + 8, 8), C), :] = q[
            pl.ds(pl.multiple_of(p * C, C), C), :
        ]

    for e in range(4):
        turn = orientation(flips[0, e])
        ghost = oriented(got[near[0, e]], turn)
        for d in range(3):
            part = ghost[d * planes : (d + 1) * planes]
            if e == 0:
                turned[pl.ds(2 - d, planes, stride=8), :] = part
            elif e == 1:
                turned[pl.ds(3 + d, planes, stride=8), :] = part
            elif e == 2:
                padded[pl.ds(7 - d, planes, stride=PAD), :] = part
            else:
                padded[pl.ds(C + 8 + d, planes, stride=PAD), :] = part
        if e in (1, 3):
            face = oriented(got_faces[near[0, e], pl.ds(3 * planes, 8), :], turn)
            if e == 1:
                faces[0:8, :] = face
            else:
                for t, field in enumerate((cour, diff)):
                    for lev in range(2):
                        j = (k * 2 + t) * 2 + lev
                        base = (t * 2 + lev) * (C + 8)
                        south[pl.ds(base, C), :] = field[0, 0, 1, lev]
                        south[pl.ds(base + C, 8), :] = jnp.broadcast_to(face[j : j + 1], (8, C))
    for g in range(groups):
        ghosts[pl.ds(g * C, C), :] = turned[pl.ds(g * C, C), :].T
    faces[...] = faces[...].T

    lane8 = lanes(8)

    @pl.loop(0, C // 8)
    def _(r):
        at = pl.multiple_of(r * 8, 8)
        east = faces[pl.ds(at, 8), :]
        for lev in range(2):
            low_x, high_x, low_y, high_y = [], [], [], []
            for t, field in enumerate((cour, diff)):
                j = (k * 2 + t) * 2 + lev
                west = field[0, 0, 0, lev, pl.ds(at, 8), :]
                low_x.append(west)
                high_x.append(
                    jnp.where(
                        lane8 == C - 1, pltpu.roll(east, C - 1 - j, 1), pltpu.roll(west, C - 1, 1)
                    )
                )
                base = (t * 2 + lev) * (C + 8)
                low_y.append(south[pl.ds(base + at, 8), :])
                high_y.append(south[pl.ds(base + at + 1, 8), :])
            along_x = stencil(taps(*low_x), taps(*high_x))
            along_y = stencil(taps(*low_y), taps(*high_y))
            centre = 1.0 + along_x[3] + along_y[3]
            every = [centre] + along_x[:3] + along_x[4:] + along_y[:3] + along_y[4:]
            for i, value in enumerate(every):
                coef[lev * 13 + i, pl.ds(at, 8), :] = value

    @pl.loop(0, C // 8)
    def _(r):
        at = pl.multiple_of(r * 8, 8)
        for lev in range(2):
            w = [coef[lev * 13 + i, pl.ds(at, 8), :] for i in range(13)]
            for s in range(planes // 2):
                p = 2 * s + lev
                base = p * PAD + 8 + at
                mid = padded[pl.ds(base, 8), :]
                edge = ghosts[pl.ds((p // 16) * C + at, 8), :]
                edge = pltpu.roll(edge, C - (8 * (p % 16) + 3), 1)
                total = w[0] * mid
                for i, d in enumerate((3, 2, 1)):
                    total += w[1 + i] * pltpu.roll(
                        jnp.where(lane8 >= C - d, edge, mid), d, 1
                    )
                    total += w[7 + i] * padded[pl.ds(base - d, 8), :]
                for i, d in enumerate((1, 2, 3)):
                    total += w[4 + i] * pltpu.roll(
                        jnp.where(lane8 < d, edge, mid), C - d, 1
                    )
                    total += w[10 + i] * padded[pl.ds(base + d, 8), :]
                out[pl.ds(p * C + at, 8), :] = total

    if not last:
        pack_strips(planes, out, strips, turned)
        fill_slots(sizes["tile"], near, strips, slots)


def advance(sizes, k, last, roots, near, flips, q, cour_all, diff_all, got_faces, got):
    planes = q.shape[0] // C
    n = sizes["tile"]
    rows = 3 * planes
    out_shape = [jax.ShapeDtypeStruct(q.shape, q.dtype)]
    out_specs = [whole_spec(q.shape)]
    groups = groups_of(planes)
    scratch = [
        pltpu.VMEM((planes * PAD, C), jnp.float32),
        pltpu.VMEM((groups * C, C), jnp.float32),
        pltpu.VMEM((groups * C, C), jnp.float32),
        pltpu.VMEM((26, C, C), jnp.float32),
        pltpu.VMEM((4 * (C + 8), C), jnp.float32),
        pltpu.VMEM((C, C), jnp.float32),
    ]
    if not last:
        out_shape.append(jax.ShapeDtypeStruct((n, rows, C), q.dtype))
        out_specs.append(whole_spec((n, rows, C)))
        scratch.append(pltpu.VMEM((4, rows, C), jnp.float32))
    return pl.pallas_call(
        functools.partial(step_kernel, sizes, planes, k, last),
        out_shape=out_shape,
        grid_spec=pltpu.PrefetchScalarGridSpec(
            num_scalar_prefetch=3,
            grid=(1,),
            in_specs=[
                whole_spec(q.shape),
                field_spec(k),
                field_spec(k),
                whole_spec(got_faces.shape),
                whole_spec(got.shape),
            ],
            out_specs=out_specs,
            scratch_shapes=scratch,
        ),
        compiler_params=pltpu.CompilerParams(vmem_limit_bytes=VMEM_LIMIT),
        name=f"advance_{k}",
    )(roots, near, flips, q, cour_all, diff_all, got_faces, got)


def body(sizes, tracers, courant, diffusivity, edge_blocks, edge_flips, roots):
    q = tracers.reshape(-1, C)
    cour_all, diff_all = spread_fields(sizes, courant, diffusivity)
    slots = pack_first(sizes, roots, edge_blocks, q, cour_all, diff_all)
    first = swap_slots(sizes, slots, 0)
    q, slots = advance(
        sizes, 0, False, roots, edge_blocks, edge_flips, q, cour_all, diff_all, first, first
    )
    second = swap_slots(sizes, slots, 1)
    (q,) = advance(
        sizes, 1, True, roots, edge_blocks, edge_flips, q, cour_all, diff_all, first, second
    )
    return q.reshape(tracers.shape)


def solution(mesh):
    placed = (
        P("spec", None, "tile", None),
        P("spec", None, None, None, "tile", None),
        P("spec", None, None, None, "tile", None),
        P("tile", None),
        P("tile", None),
        P(None, "tile"),
    )
    return jax.shard_map(
        functools.partial(body, dict(mesh.shape)),
        mesh=mesh,
        in_specs=placed,
        out_specs=P("spec", None, "tile", None),
        check_vma=False,
    )
```

time: 390 us -> 197 us (0.51)
  the two profiles are of different devices: /device:TPU:0 before, /device:TPU:14 now
where the time goes in v1:
time: 197 us; the launch traced here: 196 us
  Pallas kernels  195 us (99%)
    pallas_call x2, Pallas kernels, advance(): pl.pallas_call(functools.partial(step_kernel, sizes, planes, k, last), ou...  91.5 us
    pallas_call x2, Pallas kernels, swap_slots(): pl.pallas_call(functools.partial(swap_kernel, sizes), out_shape=jax.Shape...  65.2 us
    pallas_call x1, Pallas kernels, spread_fields(): pl.pallas_call(functools.partial(spread_kernel, sizes), out_shape=(shape,...  33 us
    pallas_call x1, Pallas kernels, pack_first(): pl.pallas_call(functools.partial(pack_kernel, sizes, planes), out_shape=j...  5.32 us

profile of v1, /device:TPU:14, one launch (start us, length us, event | category | flops | bytes accessed | tf_op | source)
XLA Modules:
  0.0 196.4 jit_solution(16071489272221136110)
XLA Ops:
  0.0 1.3 copy.9.roots
  1.3 33.0 %spread_fields.1 = (f32[2,2,2,2,128,128]{5,4,3,2,1,0:T(8,128)}, f32[2,2,2,2,128,128]{5,4,3,2,1,0:T(8,128)}) custom-call(f32[1,2,2,2,128,128]{5,4,3,2,1,0:T(8,128)} %cour.1, f32[1,2,2,2,128,128]{5,4,3,2,1,0:T(8,128)} %diff.1), custom_call_target="tpu_custom_call" | custom-call | tf_op jit(solution)/shard_map/spread_fields/pallas_call | solution.py:98
  34.3 5.3 %pack_first.1.slots = f32[16,152,128]{2,1,0:T(8,128)} custom-call(s32[2,1]{1,0:T(2,128)} %copy.9.roots, s32[1,4]{1,0:T(1,128)} %near.5, f32[6144,128]{1,0:T(8,128)} %bitcast.2, f32[2,2,2,2,128,128]{5,4,3,2,1,0:T(8,128)} %get-tuple-element.9.cour0.cour1.cour, f32[2,2,2,2,128,128]{5,4,3,2,1,0:T(8,128)} %get-tuple-element.9.cour0.cour1.cour, ...), custom_call_target="tpu_custom_call" | custom-call | tf_op jit(solution)/shard_map/pack_first/pallas_call | solution.py:192
  39.6 34.7 %swap_slots_0.1.got_faces.got = f32[16,152,128]{2,1,0:T(8,128)} custom-call(f32[16,152,128]{2,1,0:T(8,128)} %pack_first.1.slots), custom_call_target="tpu_custom_call" | custom-call | tf_op jit(solution)/shard_map/swap_slots_0/pallas_call | solution.py:116
  74.3 46.7 %advance_0.1 = (f32[6144,128]{1,0:T(8,128)}, f32[16,144,128]{2,1,0:T(8,128)}) custom-call(s32[2,1]{1,0:T(2,128)} %copy.9.roots, s32[1,4]{1,0:T(1,128)} %near.5, s32[1,4]{1,0:T(1,128)} %flips.3, f32[6144,128]{1,0:T(8,128)} %bitcast.3, f32[2,2,2,2,128,128]{5,4,3,2,1,0:T(8,128)} %get-tuple-element.9.cour0.cour1.cour, ...), custom_call_target="tpu_custom_call" | custom-call | tf_op jit(solution)/shard_map/advance_0/pallas_call | solution.py:379
  121.0 30.6 %swap_slots_1.1.got = f32[16,144,128]{2,1,0:T(8,128)} custom-call(f32[16,144,128]{2,1,0:T(8,128)} %get-tuple-element.12.slots), custom_call_target="tpu_custom_call" | custom-call | tf_op jit(solution)/shard_map/swap_slots_1/pallas_call | solution.py:116
  151.6 44.8 %advance_1.1 = f32[6144,128]{1,0:T(8,128)} custom-call(s32[2,1]{1,0:T(2,128)} %copy.9.roots, s32[1,4]{1,0:T(1,128)} %near.5, s32[1,4]{1,0:T(1,128)} %flips.3, f32[6144,128]{1,0:T(8,128)} %get-tuple-element.11.q, f32[2,2,2,2,128,128]{5,4,3,2,1,0:T(8,128)} %get-tuple-element.9.cour0.cour1.cour, f32[2,2,2,2,128,128]{5,4,3,2,1,0:T(8,128)} %get-tuple-element.10.diff0.diff1.diff, ...), custom_call_target="tpu_custom_call" | custom-call | tf_op jit(solution)/shard_map/advance_1/pallas_call | solution.py:379

commit v2 on v1

--- a/solution.py
+++ b/solution.py
@@ -1,4 +1,5 @@
 import functools
+import math
 
 import jax
 import jax.numpy as jnp
@@ -27,14 +28,10 @@
     pl.semaphore_wait(barrier, n - 1)
 
 
-def spread_kernel(sizes, cour, diff, cour_all, diff_all, send_sem, recv_sem, own_sem):
+def spread_kernel(sizes, cour, diff, cour_all, diff_all, send_sem, recv_sem):
     n = sizes["spec"]
     me = lax.axis_index("spec")
     greet_all(sizes, "spec")
-    own = [
-        pltpu.make_async_copy(cour.at[0], cour_all.at[me], own_sem.at[0]),
-        pltpu.make_async_copy(diff.at[0], diff_all.at[me], own_sem.at[1]),
-    ]
 
     def copies(off):
         peer = lax.rem(me + off, n)
@@ -55,11 +52,6 @@
         for copy in copies(off):
             copy.start()
 
-    for copy in own:
-        copy.start()
-    for copy in own:
-        copy.wait()
-
     @pl.loop(1, n)
     def _(off):
         for copy in copies(off):
@@ -103,7 +95,6 @@
         scratch_shapes=[
             pltpu.SemaphoreType.DMA((2, n)),
             pltpu.SemaphoreType.DMA((2, n)),
-            pltpu.SemaphoreType.DMA((2,)),
         ],
         compiler_params=pltpu.CompilerParams(collective_id=0, has_side_effects=True),
         name="spread_fields",
@@ -157,18 +148,25 @@
         slots[dest] = strips[edge]
 
 
-def pack_kernel(sizes, planes, roots, near, q, cour0, cour1, diff0, diff1, slots, strips, turned):
+def pack_kernel(
+    sizes, planes, roots, near, here, q, own_c, own_d, got_c0, got_c1, got_d0, got_d1,
+    slots, fields, strips, turned
+):
     pack_strips(planes, q, strips, turned)
     lane = lanes(C)
     faces = jnp.zeros((C, C), jnp.float32)
-    for k, fields in enumerate([(cour0, diff0), (cour1, diff1)]):
-        for t, field in enumerate(fields):
+    for k, got in enumerate([(got_c0, got_d0), (got_c1, got_d1)]):
+        mine = roots[k, 0] == here[0]
+        for t, own in enumerate((own_c, own_d)):
             for lev in range(2):
                 j = (k * 2 + t) * 2 + lev
-                west = field[0, 0, 0, lev]
+                west = jnp.where(mine, own[0, k, 0, lev], got[t][0, 0, 0, lev])
+                low = jnp.where(mine, own[0, k, 1, lev], got[t][0, 0, 1, lev])
+                fields[k, t, 0, lev] = west
+                fields[k, t, 1, lev] = low
                 west = pltpu.roll(west, j, 1) if j else west
                 faces = jnp.where(lane == j, west, faces)
-                strips[2, pl.ds(3 * planes + j, 1), :] = field[0, 0, 1, lev, 0:1, :]
+                strips[2, pl.ds(3 * planes + j, 1), :] = low[0:1, :]
     strips[0, pl.ds(3 * planes, 8), :] = faces.T[0:8]
     strips[1, pl.ds(3 * planes, 8), :] = jnp.zeros((8, C), jnp.float32)
     strips[3, pl.ds(3 * planes, 8), :] = jnp.zeros((8, C), jnp.float32)
@@ -185,24 +183,29 @@
     return pl.BlockSpec(shape, lambda i, *_: (0,) * len(shape))
 
 
-def pack_first(sizes, roots, near, q, cour_all, diff_all):
+def pack_first(sizes, roots, near, q, cour, diff, cour_all, diff_all):
     planes = q.shape[0] // C
     n = sizes["tile"]
     rows = 3 * planes + 8
     return pl.pallas_call(
         functools.partial(pack_kernel, sizes, planes),
-        out_shape=jax.ShapeDtypeStruct((n, rows, C), jnp.float32),
+        out_shape=(
+            jax.ShapeDtypeStruct((n, rows, C), jnp.float32),
+            jax.ShapeDtypeStruct((2, 2, 2, 2, C, C), jnp.float32),
+        ),
         grid_spec=pltpu.PrefetchScalarGridSpec(
-            num_scalar_prefetch=2,
+            num_scalar_prefetch=3,
             grid=(1,),
             in_specs=[
                 whole_spec(q.shape),
+                whole_spec(cour.shape),
+                whole_spec(diff.shape),
                 field_spec(0),
                 field_spec(1),
                 field_spec(0),
                 field_spec(1),
             ],
-            out_specs=whole_spec((n, rows, C)),
+            out_specs=(whole_spec((n, rows, C)), whole_spec((2, 2, 2, 2, C, C))),
             scratch_shapes=[
                 pltpu.VMEM((4, rows, C), jnp.float32),
                 pltpu.VMEM((groups_of(planes) * C, C), jnp.float32),
@@ -210,7 +213,18 @@
         ),
         compiler_params=pltpu.CompilerParams(vmem_limit_bytes=VMEM_LIMIT),
         name="pack_first",
-    )(roots, near, q, cour_all, cour_all, diff_all, diff_all)
+    )(
+        roots,
+        near,
+        lax.axis_index("spec").reshape(1),
+        q,
+        cour,
+        diff,
+        cour_all,
+        cour_all,
+        diff_all,
+        diff_all,
+    )
 
 
 def orientation(flipped):
@@ -258,21 +272,50 @@
     return result
 
 
-def step_kernel(
-    sizes, planes, k, last, roots, near, flips, q, cour, diff, got_faces, got, *rest
-):
+def chunk_of(planes):
+    return math.gcd(planes, 16)
+
+
+SHIFTS = (-3, -2, -1, 1, 2, 3)
+
+
+def shift_weights(weights):
+    row = lax.broadcasted_iota(jnp.int32, (3 * C, C), 0)
+    col = lax.broadcasted_iota(jnp.int32, (3 * C, C), 1)
+    item = row & 7
+    outside = jnp.where(item < 3, item - 3, C - 3 + item)
+    outside = jnp.where((row < 2 * C + 16) & (item < 6), outside, -C)
+    source = jnp.where(row < 2 * C, row & (C - 1), outside)
+    for i, shift in enumerate(SHIFTS):
+        weights[:, i * C : (i + 1) * C] = jnp.where(source == col + shift, 1.0, 0.0).astype(
+            jnp.bfloat16
+        )
+
+
+def halves(x):
+    big = x.astype(jnp.bfloat16)
+    return big, (x - big.astype(jnp.float32)).astype(jnp.bfloat16)
+
+
+def step_kernel(sizes, planes, k, last, near, flips, q, fields, got_faces, got, *rest):
     if last:
-        out, padded, turned, ghosts, coef, south, faces = rest
+        out, padded, turned, coef, south, faces, split, weights, moved = rest
     else:
-        out, slots, padded, turned, ghosts, coef, south, faces, strips = rest
+        out, slots, padded, turned, coef, south, faces, split, weights, moved, strips = rest
     groups = groups_of(planes)
+    chunk = chunk_of(planes)
+    shift_weights(weights)
 
     @pl.loop(0, planes)
     def _(p):
-        padded[pl.ds(pl.multiple_of(p * PAD + 8, 8), C), :] = q[
-            pl.ds(pl.multiple_of(p * C, C), C), :
-        ]
-
+        at = pl.multiple_of(p * C, C)
+        plane = q[pl.ds(at, C), :]
+        padded[pl.ds(pl.multiple_of(p * PAD + 8, 8), C), :] = plane
+        big, small = halves(plane)
+        split[pl.ds(at, C), 0:C] = big
+        split[pl.ds(at, C), C : 2 * C] = small
+
+    turned[...] = jnp.zeros_like(turned)
     for e in range(4):
         turn = orientation(flips[0, e])
         ghost = oriented(got[near[0, e]], turn)
@@ -289,17 +332,32 @@
         if e in (1, 3):
             face = oriented(got_faces[near[0, e], pl.ds(3 * planes, 8), :], turn)
             if e == 1:
+                faces[...] = jnp.zeros_like(faces)
                 faces[0:8, :] = face
             else:
-                for t, field in enumerate((cour, diff)):
+                for t in range(2):
                     for lev in range(2):
                         j = (k * 2 + t) * 2 + lev
                         base = (t * 2 + lev) * (C + 8)
-                        south[pl.ds(base, C), :] = field[0, 0, 1, lev]
+                        south[pl.ds(base, C), :] = fields[0, t, 1, lev]
                         south[pl.ds(base + C, 8), :] = jnp.broadcast_to(face[j : j + 1], (8, C))
-    for g in range(groups):
-        ghosts[pl.ds(g * C, C), :] = turned[pl.ds(g * C, C), :].T
     faces[...] = faces[...].T
+
+    row = lax.broadcasted_iota(jnp.int32, (2 * C, C), 0)
+    col = lax.broadcasted_iota(jnp.int32, (2 * C, C), 1)
+    source = (row & 7) + 8 * (row // C)
+    ghosts = [
+        jnp.concatenate(halves(turned[pl.ds(g * C, C), :].T), axis=1) for g in range(groups)
+    ]
+    for slot in range(min(16, planes)):
+        place = jnp.where((((row & (C - 1)) >> 3) == slot) & (source == col), 1.0, 0.0)
+        place = place.astype(jnp.bfloat16)
+        for g in range(groups):
+            p = 16 * g + slot
+            if p < planes:
+                split[pl.ds(p * C, C), 2 * C : 3 * C] = jnp.dot(
+                    ghosts[g], place, preferred_element_type=jnp.float32
+                ).astype(jnp.bfloat16)
 
     lane8 = lanes(8)
 
@@ -309,9 +367,9 @@
         east = faces[pl.ds(at, 8), :]
         for lev in range(2):
             low_x, high_x, low_y, high_y = [], [], [], []
-            for t, field in enumerate((cour, diff)):
+            for t in range(2):
                 j = (k * 2 + t) * 2 + lev
-                west = field[0, 0, 0, lev, pl.ds(at, 8), :]
+                west = fields[0, t, 0, lev, pl.ds(at, 8), :]
                 low_x.append(west)
                 high_x.append(
                     jnp.where(
@@ -328,36 +386,39 @@
             for i, value in enumerate(every):
                 coef[lev * 13 + i, pl.ds(at, 8), :] = value
 
-    @pl.loop(0, C // 8)
-    def _(r):
-        at = pl.multiple_of(r * 8, 8)
-        for lev in range(2):
-            w = [coef[lev * 13 + i, pl.ds(at, 8), :] for i in range(13)]
-            for s in range(planes // 2):
-                p = 2 * s + lev
-                base = p * PAD + 8 + at
-                mid = padded[pl.ds(base, 8), :]
-                edge = ghosts[pl.ds((p // 16) * C + at, 8), :]
-                edge = pltpu.roll(edge, C - (8 * (p % 16) + 3), 1)
-                total = w[0] * mid
-                for i, d in enumerate((3, 2, 1)):
-                    total += w[1 + i] * pltpu.roll(
-                        jnp.where(lane8 >= C - d, edge, mid), d, 1
-                    )
-                    total += w[7 + i] * padded[pl.ds(base - d, 8), :]
-                for i, d in enumerate((1, 2, 3)):
-                    total += w[4 + i] * pltpu.roll(
-                        jnp.where(lane8 < d, edge, mid), C - d, 1
-                    )
-                    total += w[10 + i] * padded[pl.ds(base + d, 8), :]
-                out[pl.ds(p * C + at, 8), :] = total
+    @pl.loop(0, planes // chunk)
+    def _(part):
+        rows = min(4, chunk) * C
+
+        @pl.loop(0, chunk * C // rows)
+        def _(b):
+            at = pl.multiple_of(part * (chunk * C) + b * rows, C)
+            moved[pl.ds(pl.multiple_of(b * rows, C), rows), :] = jnp.dot(
+                split[pl.ds(at, rows), :], weights[...], preferred_element_type=jnp.float32
+            )
+
+        @pl.loop(0, C // 8)
+        def _(r):
+            at = pl.multiple_of(r * 8, 8)
+            for lev in range(2):
+                w = [coef[lev * 13 + i, pl.ds(at, 8), :] for i in range(13)]
+                for s in range(chunk // 2):
+                    p = 2 * s + lev
+                    base = (part * chunk + p) * PAD + 8 + at
+                    here = pl.ds(pl.multiple_of(p * C + at, 8), 8)
+                    total = w[0] * padded[pl.ds(base, 8), :]
+                    for i, d in enumerate(SHIFTS):
+                        total += w[1 + i] * moved[here, i * C : (i + 1) * C]
+                        total += w[7 + i] * padded[pl.ds(base + d, 8), :]
+                    to = pl.multiple_of((part * chunk + p) * C + at, 8)
+                    out[pl.ds(to, 8), :] = total
 
     if not last:
         pack_strips(planes, out, strips, turned)
         fill_slots(sizes["tile"], near, strips, slots)
 
 
-def advance(sizes, k, last, roots, near, flips, q, cour_all, diff_all, got_faces, got):
+def advance(sizes, k, last, near, flips, q, fields, got_faces, got):
     planes = q.shape[0] // C
     n = sizes["tile"]
     rows = 3 * planes
@@ -367,10 +428,12 @@
     scratch = [
         pltpu.VMEM((planes * PAD, C), jnp.float32),
         pltpu.VMEM((groups * C, C), jnp.float32),
-        pltpu.VMEM((groups * C, C), jnp.float32),
         pltpu.VMEM((26, C, C), jnp.float32),
         pltpu.VMEM((4 * (C + 8), C), jnp.float32),
         pltpu.VMEM((C, C), jnp.float32),
+        pltpu.VMEM((planes * C, 3 * C), jnp.bfloat16),
+        pltpu.VMEM((3 * C, 6 * C), jnp.bfloat16),
+        pltpu.VMEM((chunk_of(planes) * C, 6 * C), jnp.float32),
     ]
     if not last:
         out_shape.append(jax.ShapeDtypeStruct((n, rows, C), q.dtype))
@@ -380,12 +443,11 @@
         functools.partial(step_kernel, sizes, planes, k, last),
         out_shape=out_shape,
         grid_spec=pltpu.PrefetchScalarGridSpec(
-            num_scalar_prefetch=3,
+            num_scalar_prefetch=2,
             grid=(1,),
             in_specs=[
                 whole_spec(q.shape),
-                field_spec(k),
-                field_spec(k),
+                pl.BlockSpec((1, 2, 2, 2, C, C), lambda i, *_: (k, 0, 0, 0, 0, 0)),
                 whole_spec(got_faces.shape),
                 whole_spec(got.shape),
             ],
@@ -394,21 +456,19 @@
         ),
         compiler_params=pltpu.CompilerParams(vmem_limit_bytes=VMEM_LIMIT),
         name=f"advance_{k}",
-    )(roots, near, flips, q, cour_all, diff_all, got_faces, got)
+    )(near, flips, q, fields, got_faces, got)
 
 
 def body(sizes, tracers, courant, diffusivity, edge_blocks, edge_flips, roots):
     q = tracers.reshape(-1, C)
     cour_all, diff_all = spread_fields(sizes, courant, diffusivity)
-    slots = pack_first(sizes, roots, edge_blocks, q, cour_all, diff_all)
+    slots, fields = pack_first(
+        sizes, roots, edge_blocks, q, courant, diffusivity, cour_all, diff_all
+    )
     first = swap_slots(sizes, slots, 0)
-    q, slots = advance(
-        sizes, 0, False, roots, edge_blocks, edge_flips, q, cour_all, diff_all, first, first
-    )
+    q, slots = advance(sizes, 0, False, edge_blocks, edge_flips, q, fields, first, first)
     second = swap_slots(sizes, slots, 1)
-    (q,) = advance(
-        sizes, 1, True, roots, edge_blocks, edge_flips, q, cour_all, diff_all, first, second
-    )
+    (q,) = advance(sizes, 1, True, edge_blocks, edge_flips, q, fields, first, second)
     return q.reshape(tracers.shape)
 
 

time: 197 us -> 117 us (0.59)
  Pallas kernels: 195 us -> 115 us
    pallas_call x2, Pallas kernels: 91.5 us -> 41.7 us  [advance(): pl.pallas_call(functools.partial(step_kernel, sizes, planes, k, last), ou...]
    pallas_call x1, Pallas kernels: 33 us -> 3.07 us  [spread_fields(): pl.pallas_call(functools.partial(spread_kernel, sizes), out_shape=(shape,...]
where the time goes in v2:
time: 117 us
  Pallas kernels  115 us (98%)
  local copies, waits for them, and re-layouts  1.26 us (1%)
    pallas_call x2, Pallas kernels, swap_slots(): pl.pallas_call(functools.partial(swap_kernel, sizes), out_shape=jax.Shape...  64.6 us
    pallas_call x2, Pallas kernels, advance(): pl.pallas_call(functools.partial(step_kernel, sizes, planes, k, last), ou...  41.7 us
    pallas_call x1, Pallas kernels, pack_first(): pl.pallas_call(functools.partial(pack_kernel, sizes, planes), out_shape=(...  6.08 us
    pallas_call x1, Pallas kernels, spread_fields(): pl.pallas_call(functools.partial(spread_kernel, sizes), out_shape=(shape,...  3.07 us

profile of v2, /device:TPU:14, one launch (start us, length us, event | category | flops | bytes accessed | tf_op | source)
XLA Modules:
  0.0 116.8 jit_solution(14118655351525568372)
XLA Ops:
  0.0 1.3 %copy.7.roots = s32[2,1]{1,0:T(2,128)} copy(s32[2,1]{0,1:T(1,128)} %param.11) | data formatting | bytes 16 | tf_op args[5]
  1.3 3.1 %spread_fields.1 = (f32[2,2,2,2,128,128]{5,4,3,2,1,0:T(8,128)}, f32[2,2,2,2,128,128]{5,4,3,2,1,0:T(8,128)}) custom-call(f32[1,2,2,2,128,128]{5,4,3,2,1,0:T(8,128)} %own_c.1, f32[1,2,2,2,128,128]{5,4,3,2,1,0:T(8,128)} %own_d.1), custom_call_target="tpu_custom_call" | custom-call | tf_op jit(solution)/shard_map/spread_fields/pallas_call | solution.py:90
  4.3 6.1 %pack_first.1 = (f32[16,152,128]{2,1,0:T(8,128)}, f32[2,2,2,2,128,128]{5,4,3,2,1,0:T(8,128)}) custom-call(s32[2,1]{1,0:T(2,128)} %copy.7.roots, s32[1,4]{1,0:T(1,128)} %near.5, s32[1]{0:T(128)} %bitcast.1.here, f32[6144,128]{1,0:T(8,128)} %bitcast.3, f32[1,2,2,2,128,128]{5,4,3,2,1,0:T(8,128)} %own_c.1, f32[1,2,2,2,128,128]{5,4,3,2,1,0:T(8,128)} %own_d.1, ...), custom_call_target="tpu_custom_call" | custom-call | tf_op jit(solution)/shard_map/pack_first/pallas_call | solution.py:190
  10.4 34.0 %swap_slots_0.1.got_faces.got = f32[16,152,128]{2,1,0:T(8,128)} custom-call(f32[16,152,128]{2,1,0:T(8,128)} %get-tuple-element.14.slots), custom_call_target="tpu_custom_call" | custom-call | tf_op jit(solution)/shard_map/swap_slots_0/pallas_call | solution.py:107
  44.4 21.9 %advance_0.1 = (f32[6144,128]{1,0:T(8,128)}, f32[16,144,128]{2,1,0:T(8,128)}) custom-call(s32[1,4]{1,0:T(1,128)} %near.5, s32[1,4]{1,0:T(1,128)} %flips.3, f32[6144,128]{1,0:T(8,128)} %bitcast.4, f32[2,2,2,2,128,128]{5,4,3,2,1,0:T(8,128)} %get-tuple-element.13.fields, f32[16,152,128]{2,1,0:T(8,128)} %swap_slots_0.1.got_faces.got, ...), custom_call_target="tpu_custom_call" | custom-call | tf_op jit(solution)/shard_map/advance_0/pallas_call | solution.py:442
  66.2 30.7 %swap_slots_1.1.got = f32[16,144,128]{2,1,0:T(8,128)} custom-call(f32[16,144,128]{2,1,0:T(8,128)} %get-tuple-element.16.slots), custom_call_target="tpu_custom_call" | custom-call | tf_op jit(solution)/shard_map/swap_slots_1/pallas_call | solution.py:107
  96.9 19.9 %advance_1.1 = f32[6144,128]{1,0:T(8,128)} custom-call(s32[1,4]{1,0:T(1,128)} %near.5, s32[1,4]{1,0:T(1,128)} %flips.3, f32[6144,128]{1,0:T(8,128)} %get-tuple-element.15.q, f32[2,2,2,2,128,128]{5,4,3,2,1,0:T(8,128)} %get-tuple-element.13.fields, f32[16,152,128]{2,1,0:T(8,128)} %swap_slots_0.1.got_faces.got, f32[16,144,128]{2,1,0:T(8,128)} %swap_slots_1.1.got), custom_call_target="tpu_custom_call" | custom-call | tf_op jit(solution)/shard_map/advance_1/pallas_call | solution.py:442

commit v3 on v2

--- a/solution.py
+++ b/solution.py
@@ -58,29 +58,97 @@
             copy.wait()
 
 
-def swap_kernel(sizes, slots, got, send_sem, recv_sem):
+def swap_kernel(
+    sizes, slots, strips, got, theirs, relay, far_sem, send_sem, recv_sem, send_on, recv_on, own_sem
+):
     n = sizes["tile"]
+    half = n // 2
+    rows = slots.shape[1]
     me = lax.axis_index("tile")
-    greet_all(sizes, "tile")
-
-    def copy_to(off):
-        peer = lax.rem(me + off, n)
+    place = lax.rem(me, half)
+    base = me - place
+    far = lax.rem(me + half, n)
+    barrier = pltpu.get_barrier_semaphore()
+    pl.semaphore_signal(barrier, inc=1, device_id={"tile": far}, device_id_type=MESH)
+
+    @pl.loop(1, half)
+    def _(off):
+        pl.semaphore_signal(
+            barrier,
+            inc=1,
+            device_id={"tile": base + lax.rem(place + off, half)},
+            device_id_type=MESH,
+        )
+
+    pl.semaphore_wait(barrier, half)
+
+    across = pltpu.make_async_remote_copy(
+        src_ref=strips,
+        dst_ref=theirs,
+        send_sem=far_sem.at[0],
+        recv_sem=far_sem.at[1],
+        device_id={"tile": far},
+        device_id_type=MESH,
+    )
+
+    def direct(off):
+        to = lax.rem(place + off, half)
         return pltpu.make_async_remote_copy(
-            src_ref=slots.at[peer],
+            src_ref=slots.at[to],
             dst_ref=got.at[me],
             send_sem=send_sem.at[off],
             recv_sem=recv_sem.at[off],
-            device_id={"tile": peer},
+            device_id={"tile": base + to},
             device_id_type=MESH,
         )
 
-    @pl.loop(1, n)
-    def _(off):
-        copy_to(off).start()
-
-    @pl.loop(1, n)
-    def _(off):
-        copy_to(off).wait()
+    def onward(off):
+        to = lax.rem(place + off, half)
+        return pltpu.make_async_remote_copy(
+            src_ref=relay.at[to],
+            dst_ref=got.at[far],
+            send_sem=send_on.at[off],
+            recv_sem=recv_on.at[off],
+            device_id={"tile": base + to},
+            device_id_type=MESH,
+        )
+
+    def choose(to):
+        wanted = (base + to).astype(jnp.float32)
+        masks = [theirs[e, pl.ds(rows, 8), :] == wanted for e in range(1, 4)]
+
+        @pl.loop(0, rows // 8)
+        def _(r):
+            at = pl.ds(pl.multiple_of(r * 8, 8), 8)
+            value = theirs[0, at, :]
+            for e, mask in enumerate(masks):
+                value = jnp.where(mask, theirs[e + 1, at, :], value)
+            relay[to, at, :] = value
+
+    across.start()
+
+    @pl.loop(1, half)
+    def _(off):
+        direct(off).start()
+
+    across.wait_recv()
+
+    @pl.loop(1, half)
+    def _(off):
+        choose(lax.rem(place + off, half))
+        onward(off).start()
+
+    choose(place)
+    own = pltpu.make_async_copy(relay.at[place], got.at[far], own_sem)
+    own.start()
+    across.wait_send()
+
+    @pl.loop(1, half)
+    def _(off):
+        direct(off).wait()
+        onward(off).wait()
+
+    own.wait()
 
 
 def spread_fields(sizes, cour, diff):
@@ -101,18 +169,32 @@
     )(cour, diff)
 
 
-def swap_slots(sizes, slots, which):
+def swap_slots(sizes, slots, strips, which):
     n = sizes["tile"]
+    half, rows = slots.shape[0], slots.shape[1]
     anywhere = pl.BlockSpec(memory_space=pl.ANY)
     return pl.pallas_call(
         functools.partial(swap_kernel, sizes),
-        out_shape=jax.ShapeDtypeStruct(slots.shape, slots.dtype),
-        in_specs=[anywhere],
+        out_shape=jax.ShapeDtypeStruct((n, rows, C), slots.dtype),
+        in_specs=[anywhere, anywhere],
         out_specs=anywhere,
-        scratch_shapes=[pltpu.SemaphoreType.DMA((n,)), pltpu.SemaphoreType.DMA((n,))],
+        scratch_shapes=[
+            pltpu.VMEM(strips.shape, jnp.float32),
+            pltpu.VMEM(slots.shape, jnp.float32),
+            pltpu.SemaphoreType.DMA((2,)),
+            pltpu.SemaphoreType.DMA((half,)),
+            pltpu.SemaphoreType.DMA((half,)),
+            pltpu.SemaphoreType.DMA((half,)),
+            pltpu.SemaphoreType.DMA((half,)),
+            pltpu.SemaphoreType.DMA,
+        ],
         compiler_params=pltpu.CompilerParams(collective_id=1 + which, has_side_effects=True),
         name=f"swap_slots_{which}",
-    )(slots)
+    )(slots, strips)
+
+
+def rows_of(planes, faces):
+    return -(-(3 * planes + faces) // 8) * 8
 
 
 def groups_of(planes):
@@ -139,18 +221,24 @@
         strips[3, rows, :] = q[pl.ds(C - 1 - d, planes, stride=C), :]
 
 
-def fill_slots(n, near, strips, slots):
-    @pl.loop(0, n)
-    def _(dest):
+def fill_slots(near, here, strips, slots):
+    rows = slots.shape[1]
+    for e in range(4):
+        owner = near[0, e].astype(jnp.float32)
+        strips[e, pl.ds(rows, 8), :] = jnp.full((8, C), owner, jnp.float32)
+
+    @pl.loop(0, slots.shape[0])
+    def _(i):
+        dest = here[1] + i
         edge = jnp.int32(0)
         for e in range(1, 4):
             edge = jnp.where(near[0, e] == dest, e, edge)
-        slots[dest] = strips[edge]
+        slots[i] = strips[edge, pl.ds(0, rows), :]
 
 
 def pack_kernel(
     sizes, planes, roots, near, here, q, own_c, own_d, got_c0, got_c1, got_d0, got_d1,
-    slots, fields, strips, turned
+    slots, strips, fields, turned
 ):
     pack_strips(planes, q, strips, turned)
     lane = lanes(C)
@@ -170,7 +258,7 @@
     strips[0, pl.ds(3 * planes, 8), :] = faces.T[0:8]
     strips[1, pl.ds(3 * planes, 8), :] = jnp.zeros((8, C), jnp.float32)
     strips[3, pl.ds(3 * planes, 8), :] = jnp.zeros((8, C), jnp.float32)
-    fill_slots(sizes["tile"], near, strips, slots)
+    fill_slots(near, here, strips, slots)
 
 
 def field_spec(k):
@@ -183,14 +271,15 @@
     return pl.BlockSpec(shape, lambda i, *_: (0,) * len(shape))
 
 
-def pack_first(sizes, roots, near, q, cour, diff, cour_all, diff_all):
+def pack_first(sizes, roots, near, here, q, cour, diff, cour_all, diff_all):
     planes = q.shape[0] // C
-    n = sizes["tile"]
-    rows = 3 * planes + 8
+    half = sizes["tile"] // 2
+    rows = rows_of(planes, 8)
     return pl.pallas_call(
         functools.partial(pack_kernel, sizes, planes),
         out_shape=(
-            jax.ShapeDtypeStruct((n, rows, C), jnp.float32),
+            jax.ShapeDtypeStruct((half, rows, C), jnp.float32),
+            jax.ShapeDtypeStruct((4, rows + 8, C), jnp.float32),
             jax.ShapeDtypeStruct((2, 2, 2, 2, C, C), jnp.float32),
         ),
         grid_spec=pltpu.PrefetchScalarGridSpec(
@@ -205,9 +294,12 @@
                 field_spec(0),
                 field_spec(1),
             ],
-            out_specs=(whole_spec((n, rows, C)), whole_spec((2, 2, 2, 2, C, C))),
+            out_specs=(
+                whole_spec((half, rows, C)),
+                whole_spec((4, rows + 8, C)),
+                whole_spec((2, 2, 2, 2, C, C)),
+            ),
             scratch_shapes=[
-                pltpu.VMEM((4, rows, C), jnp.float32),
                 pltpu.VMEM((groups_of(planes) * C, C), jnp.float32),
             ],
         ),
@@ -216,7 +308,7 @@
     )(
         roots,
         near,
-        lax.axis_index("spec").reshape(1),
+        here,
         q,
         cour,
         diff,
@@ -297,11 +389,11 @@
     return big, (x - big.astype(jnp.float32)).astype(jnp.bfloat16)
 
 
-def step_kernel(sizes, planes, k, last, near, flips, q, fields, got_faces, got, *rest):
+def step_kernel(sizes, planes, k, last, near, flips, here, q, fields, got_faces, got, *rest):
     if last:
         out, padded, turned, coef, south, faces, split, weights, moved = rest
     else:
-        out, slots, padded, turned, coef, south, faces, split, weights, moved, strips = rest
+        out, slots, strips, padded, turned, coef, south, faces, split, weights, moved = rest
     groups = groups_of(planes)
     chunk = chunk_of(planes)
     shift_weights(weights)
@@ -415,13 +507,13 @@
 
     if not last:
         pack_strips(planes, out, strips, turned)
-        fill_slots(sizes["tile"], near, strips, slots)
-
-
-def advance(sizes, k, last, near, flips, q, fields, got_faces, got):
+        fill_slots(near, here, strips, slots)
+
+
+def advance(sizes, k, last, near, flips, here, q, fields, got_faces, got):
     planes = q.shape[0] // C
-    n = sizes["tile"]
-    rows = 3 * planes
+    half = sizes["tile"] // 2
+    rows = rows_of(planes, 0)
     out_shape = [jax.ShapeDtypeStruct(q.shape, q.dtype)]
     out_specs = [whole_spec(q.shape)]
     groups = groups_of(planes)
@@ -436,14 +528,14 @@
         pltpu.VMEM((chunk_of(planes) * C, 6 * C), jnp.float32),
     ]
     if not last:
-        out_shape.append(jax.ShapeDtypeStruct((n, rows, C), q.dtype))
-        out_specs.append(whole_spec((n, rows, C)))
-        scratch.append(pltpu.VMEM((4, rows, C), jnp.float32))
+        for shape in ((half, rows, C), (4, rows + 8, C)):
+            out_shape.append(jax.ShapeDtypeStruct(shape, q.dtype))
+            out_specs.append(whole_spec(shape))
     return pl.pallas_call(
         functools.partial(step_kernel, sizes, planes, k, last),
         out_shape=out_shape,
         grid_spec=pltpu.PrefetchScalarGridSpec(
-            num_scalar_prefetch=2,
+            num_scalar_prefetch=3,
             grid=(1,),
             in_specs=[
                 whole_spec(q.shape),
@@ -456,19 +548,22 @@
         ),
         compiler_params=pltpu.CompilerParams(vmem_limit_bytes=VMEM_LIMIT),
         name=f"advance_{k}",
-    )(near, flips, q, fields, got_faces, got)
+    )(near, flips, here, q, fields, got_faces, got)
 
 
 def body(sizes, tracers, courant, diffusivity, edge_blocks, edge_flips, roots):
     q = tracers.reshape(-1, C)
     cour_all, diff_all = spread_fields(sizes, courant, diffusivity)
-    slots, fields = pack_first(
-        sizes, roots, edge_blocks, q, courant, diffusivity, cour_all, diff_all
-    )
-    first = swap_slots(sizes, slots, 0)
-    q, slots = advance(sizes, 0, False, edge_blocks, edge_flips, q, fields, first, first)
-    second = swap_slots(sizes, slots, 1)
-    (q,) = advance(sizes, 1, True, edge_blocks, edge_flips, q, fields, first, second)
+    half = sizes["tile"] // 2
+    here = jnp.stack([lax.axis_index("spec"), lax.axis_index("tile") // half * half])
+    slots, strips, fields = pack_first(
+        sizes, roots, edge_blocks, here, q, courant, diffusivity, cour_all, diff_all
+    )
+    first = swap_slots(sizes, slots, strips, 0)
+    block = (edge_blocks, edge_flips, here)
+    q, slots, strips = advance(sizes, 0, False, *block, q, fields, first, first)
+    second = swap_slots(sizes, slots, strips, 1)
+    (q,) = advance(sizes, 1, True, *block, q, fields, first, second)
     return q.reshape(tracers.shape)
 
 

time: 117 us -> 110 us (0.940); the launches traced: 117 us -> 108 us
  Pallas kernels: 115 us -> 106 us
    pallas_call x2, Pallas kernels: 64.6 us -> 55.7 us  [swap_slots(): pl.pallas_call(functools.partial(swap_kernel, sizes), out_shape=jax.Shape...]
where the time goes in v3:
time: 110 us; the launch traced here: 108 us
  Pallas kernels  106 us (96%)
  local copies, waits for them, and re-layouts  1.3 us (1%)
    pallas_call x2, Pallas kernels, swap_slots(): pl.pallas_call(functools.partial(swap_kernel, sizes), out_shape=jax.Shape...  55.7 us
    pallas_call x2, Pallas kernels, advance(): pl.pallas_call(functools.partial(step_kernel, sizes, planes, k, last), ou...  41.5 us
    pallas_call x1, Pallas kernels, pack_first(): pl.pallas_call(functools.partial(pack_kernel, sizes, planes), out_shape=(...  5.87 us
    pallas_call x1, Pallas kernels, spread_fields(): pl.pallas_call(functools.partial(spread_kernel, sizes), out_shape=(shape,...  3.07 us

profile of v3, /device:TPU:14, one launch (start us, length us, event | category | flops | bytes accessed | tf_op | source)
XLA Modules:
  0.0 108.1 jit_solution(804605982452651003)
XLA Ops:
  0.0 0.6 pad_add_fusion.here
  0.6 1.3 %copy.7.roots = s32[2,1]{1,0:T(2,128)} copy(s32[2,1]{0,1:T(1,128)} %param.11) | data formatting | bytes 16 | tf_op args[5]
  1.9 3.1 %spread_fields.1 = (f32[2,2,2,2,128,128]{5,4,3,2,1,0:T(8,128)}, f32[2,2,2,2,128,128]{5,4,3,2,1,0:T(8,128)}) custom-call(f32[1,2,2,2,128,128]{5,4,3,2,1,0:T(8,128)} %own_c.1, f32[1,2,2,2,128,128]{5,4,3,2,1,0:T(8,128)} %own_d.1), custom_call_target="tpu_custom_call" | custom-call | tf_op jit(solution)/shard_map/spread_fields/pallas_call | solution.py:158
  5.0 5.9 %pack_first.1 = (f32[8,152,128]{2,1,0:T(8,128)}, f32[4,160,128]{2,1,0:T(8,128)}, f32[2,2,2,2,128,128]{5,4,3,2,1,0:T(8,128)}) custom-call(s32[2,1]{1,0:T(2,128)} %copy.7.roots, s32[1,4]{1,0:T(1,128)} %near.5, s32[2]{0:T(128)} %pad_add_fusion.here, f32[6144,128]{1,0:T(8,128)} %bitcast.4, f32[1,2,2,2,128,128]{5,4,3,2,1,0:T(8,128)} %own_c.1, ...), custom_call_target="tpu_custom_call" | custom-call | tf_op jit(solution)/shard_map/pack_first/pallas_call | solution.py:278
  10.9 30.3 %swap_slots_0.1.got_faces.got = f32[16,152,128]{2,1,0:T(8,128)} custom-call(f32[8,152,128]{2,1,0:T(8,128)} %get-tuple-element.16.slots, f32[4,160,128]{2,1,0:T(8,128)} %get-tuple-element.17.strips), custom_call_target="tpu_custom_call" | custom-call | tf_op jit(solution)/shard_map/swap_slots_0/pallas_call | solution.py:176
  41.2 21.7 %advance_0.1 = (f32[6144,128]{1,0:T(8,128)}, f32[8,144,128]{2,1,0:T(8,128)}, f32[4,152,128]{2,1,0:T(8,128)}) custom-call(s32[1,4]{1,0:T(1,128)} %near.5, s32[1,4]{1,0:T(1,128)} %flips.3, s32[2]{0:T(128)} %pad_add_fusion.here, f32[6144,128]{1,0:T(8,128)} %bitcast.5, f32[2,2,2,2,128,128]{5,4,3,2,1,0:T(8,128)} %get-tuple-element.15.fields, ...), custom_call_target="tpu_custom_call" | custom-call | tf_op jit(solution)/shard_map/advance_0/pallas_call | solution.py:534
  62.9 25.4 %swap_slots_1.1.got = f32[16,144,128]{2,1,0:T(8,128)} custom-call(f32[8,144,128]{2,1,0:T(8,128)} %get-tuple-element.19.slots, f32[4,152,128]{2,1,0:T(8,128)} %get-tuple-element.20.strips), custom_call_target="tpu_custom_call" | custom-call | tf_op jit(solution)/shard_map/swap_slots_1/pallas_call | solution.py:176
  88.2 19.9 %advance_1.1 = f32[6144,128]{1,0:T(8,128)} custom-call(s32[1,4]{1,0:T(1,128)} %near.5, s32[1,4]{1,0:T(1,128)} %flips.3, s32[2]{0:T(128)} %pad_add_fusion.here, f32[6144,128]{1,0:T(8,128)} %get-tuple-element.18.q, f32[2,2,2,2,128,128]{5,4,3,2,1,0:T(8,128)} %get-tuple-element.15.fields, f32[16,152,128]{2,1,0:T(8,128)} %swap_slots_0.1.got_faces.got, ...), custom_call_target="tpu_custom_call" | custom-call | tf_op jit(solution)/shard_map/advance_1/pallas_call | solution.py:534

commit v4 on v3

--- a/solution.py
+++ b/solution.py
@@ -82,14 +82,20 @@
 
     pl.semaphore_wait(barrier, half)
 
-    across = pltpu.make_async_remote_copy(
-        src_ref=strips,
-        dst_ref=theirs,
-        send_sem=far_sem.at[0],
-        recv_sem=far_sem.at[1],
-        device_id={"tile": far},
-        device_id_type=MESH,
-    )
+    cut = rows // 16 * 8
+    pieces = ((cut, rows - cut, 8), (0, cut, 0))
+
+    def across(piece):
+        first, count, extra = pieces[piece]
+        part = pl.ds(first, count + extra)
+        return pltpu.make_async_remote_copy(
+            src_ref=strips.at[:, part, :],
+            dst_ref=theirs.at[:, part, :],
+            send_sem=far_sem.at[0, piece],
+            recv_sem=far_sem.at[1, piece],
+            device_id={"tile": far},
+            device_id_type=MESH,
+        )
 
     def direct(off):
         to = lax.rem(place + off, half)
@@ -102,51 +108,59 @@
             device_id_type=MESH,
         )
 
-    def onward(off):
+    def onward(piece, off):
         to = lax.rem(place + off, half)
+        part = pl.ds(*pieces[piece][:2])
         return pltpu.make_async_remote_copy(
-            src_ref=relay.at[to],
-            dst_ref=got.at[far],
-            send_sem=send_on.at[off],
-            recv_sem=recv_on.at[off],
+            src_ref=relay.at[to, part, :],
+            dst_ref=got.at[far, part, :],
+            send_sem=send_on.at[piece, off],
+            recv_sem=recv_on.at[piece, off],
             device_id={"tile": base + to},
             device_id_type=MESH,
         )
 
-    def choose(to):
+    def choose(piece, to):
+        first, count, _ = pieces[piece]
         wanted = (base + to).astype(jnp.float32)
         masks = [theirs[e, pl.ds(rows, 8), :] == wanted for e in range(1, 4)]
 
-        @pl.loop(0, rows // 8)
+        @pl.loop(0, count // 8)
         def _(r):
-            at = pl.ds(pl.multiple_of(r * 8, 8), 8)
+            at = pl.ds(pl.multiple_of(first + r * 8, 8), 8)
             value = theirs[0, at, :]
             for e, mask in enumerate(masks):
                 value = jnp.where(mask, theirs[e + 1, at, :], value)
             relay[to, at, :] = value
 
-    across.start()
+    for piece in range(2):
+        across(piece).start()
 
     @pl.loop(1, half)
     def _(off):
         direct(off).start()
 
-    across.wait_recv()
-
-    @pl.loop(1, half)
-    def _(off):
-        choose(lax.rem(place + off, half))
-        onward(off).start()
-
-    choose(place)
+    for piece in range(2):
+        across(piece).wait_recv()
+
+        @pl.loop(1, half)
+        def _(off):
+            choose(piece, lax.rem(place + off, half))
+            onward(piece, off).start()
+
+    for piece in range(2):
+        choose(piece, place)
     own = pltpu.make_async_copy(relay.at[place], got.at[far], own_sem)
     own.start()
-    across.wait_send()
+
+    for piece in range(2):
+        across(piece).wait_send()
 
     @pl.loop(1, half)
     def _(off):
         direct(off).wait()
-        onward(off).wait()
+        for piece in range(2):
+            onward(piece, off).wait()
 
     own.wait()
 
@@ -181,11 +195,11 @@
         scratch_shapes=[
             pltpu.VMEM(strips.shape, jnp.float32),
             pltpu.VMEM(slots.shape, jnp.float32),
-            pltpu.SemaphoreType.DMA((2,)),
+            pltpu.SemaphoreType.DMA((2, 2)),
             pltpu.SemaphoreType.DMA((half,)),
             pltpu.SemaphoreType.DMA((half,)),
-            pltpu.SemaphoreType.DMA((half,)),
-            pltpu.SemaphoreType.DMA((half,)),
+            pltpu.SemaphoreType.DMA((2, half)),
+            pltpu.SemaphoreType.DMA((2, half)),
             pltpu.SemaphoreType.DMA,
         ],
         compiler_params=pltpu.CompilerParams(collective_id=1 + which, has_side_effects=True),
@@ -205,20 +219,19 @@
     return lax.broadcasted_iota(jnp.int32, (rows, C), 1)
 
 
-def pack_strips(planes, q, strips, turned):
+def pack_part(planes, chunk, q, at, first, strips, turned):
     lane_group = lanes(C) // 8
-    for g in range(groups_of(planes)):
-        packed = jnp.zeros((C, C), jnp.float32)
-        for slot in range(min(16, planes - 16 * g)):
-            plane = q[pl.ds((16 * g + slot) * C, C), :]
-            packed = jnp.where(lane_group == slot, pltpu.roll(plane, 8 * slot + 3, 1), packed)
-        turned[pl.ds(g * C, C), :] = packed.T
+    packed = jnp.zeros((C, C), jnp.float32)
+    for slot in range(chunk):
+        plane = q[pl.ds((at + slot) * C, C), :]
+        packed = jnp.where(lane_group == slot, pltpu.roll(plane, 8 * slot + 3, 1), packed)
+    turned[0:C, :] = packed.T
     for d in range(3):
-        rows = pl.ds(d * planes, planes)
-        strips[0, rows, :] = turned[pl.ds(3 + d, planes, stride=8), :]
-        strips[1, rows, :] = turned[pl.ds(2 - d, planes, stride=8), :]
-        strips[2, rows, :] = q[pl.ds(d, planes, stride=C), :]
-        strips[3, rows, :] = q[pl.ds(C - 1 - d, planes, stride=C), :]
+        rows = pl.ds(first + d * planes, chunk)
+        strips[0, rows, :] = turned[pl.ds(3 + d, chunk, stride=8), :]
+        strips[1, rows, :] = turned[pl.ds(2 - d, chunk, stride=8), :]
+        strips[2, rows, :] = q[pl.ds(at * C + d, chunk, stride=C), :]
+        strips[3, rows, :] = q[pl.ds(at * C + C - 1 - d, chunk, stride=C), :]
 
 
 def fill_slots(near, here, strips, slots):
@@ -240,7 +253,9 @@
     sizes, planes, roots, near, here, q, own_c, own_d, got_c0, got_c1, got_d0, got_d1,
     slots, strips, fields, turned
 ):
-    pack_strips(planes, q, strips, turned)
+    chunk = chunk_of(planes)
+    for part in range(planes // chunk):
+        pack_part(planes, chunk, q, part * chunk, part * chunk, strips, turned)
     lane = lanes(C)
     faces = jnp.zeros((C, C), jnp.float32)
     for k, got in enumerate([(got_c0, got_d0), (got_c1, got_d1)]):
@@ -396,118 +411,122 @@
         out, slots, strips, padded, turned, coef, south, faces, split, weights, moved = rest
     groups = groups_of(planes)
     chunk = chunk_of(planes)
-    shift_weights(weights)
-
-    @pl.loop(0, planes)
-    def _(p):
+    part = pl.program_id(0)
+
+    @pl.loop(0, chunk)
+    def _(i):
+        p = part * chunk + i
         at = pl.multiple_of(p * C, C)
-        plane = q[pl.ds(at, C), :]
+        plane = q[pl.ds(pl.multiple_of(i * C, C), C), :]
         padded[pl.ds(pl.multiple_of(p * PAD + 8, 8), C), :] = plane
         big, small = halves(plane)
         split[pl.ds(at, C), 0:C] = big
         split[pl.ds(at, C), C : 2 * C] = small
 
-    turned[...] = jnp.zeros_like(turned)
-    for e in range(4):
-        turn = orientation(flips[0, e])
-        ghost = oriented(got[near[0, e]], turn)
-        for d in range(3):
-            part = ghost[d * planes : (d + 1) * planes]
-            if e == 0:
-                turned[pl.ds(2 - d, planes, stride=8), :] = part
-            elif e == 1:
-                turned[pl.ds(3 + d, planes, stride=8), :] = part
-            elif e == 2:
-                padded[pl.ds(7 - d, planes, stride=PAD), :] = part
-            else:
-                padded[pl.ds(C + 8 + d, planes, stride=PAD), :] = part
-        if e in (1, 3):
-            face = oriented(got_faces[near[0, e], pl.ds(3 * planes, 8), :], turn)
-            if e == 1:
-                faces[...] = jnp.zeros_like(faces)
-                faces[0:8, :] = face
-            else:
+    @pl.when(part == 0)
+    def _():
+        shift_weights(weights)
+        turned[...] = jnp.zeros_like(turned)
+        for e in range(4):
+            turn = orientation(flips[0, e])
+            ghost = oriented(got[near[0, e]], turn)
+            for d in range(3):
+                part = ghost[d * planes : (d + 1) * planes]
+                if e == 0:
+                    turned[pl.ds(2 - d, planes, stride=8), :] = part
+                elif e == 1:
+                    turned[pl.ds(3 + d, planes, stride=8), :] = part
+                elif e == 2:
+                    padded[pl.ds(7 - d, planes, stride=PAD), :] = part
+                else:
+                    padded[pl.ds(C + 8 + d, planes, stride=PAD), :] = part
+            if e in (1, 3):
+                face = oriented(got_faces[near[0, e], pl.ds(3 * planes, 8), :], turn)
+                if e == 1:
+                    faces[...] = jnp.zeros_like(faces)
+                    faces[0:8, :] = face
+                else:
+                    for t in range(2):
+                        for lev in range(2):
+                            j = (k * 2 + t) * 2 + lev
+                            base = (t * 2 + lev) * (C + 8)
+                            south[pl.ds(base, C), :] = fields[0, t, 1, lev]
+                            south[pl.ds(base + C, 8), :] = jnp.broadcast_to(face[j : j + 1], (8, C))
+        faces[...] = faces[...].T
+
+        row = lax.broadcasted_iota(jnp.int32, (2 * C, C), 0)
+        col = lax.broadcasted_iota(jnp.int32, (2 * C, C), 1)
+        source = (row & 7) + 8 * (row // C)
+        ghosts = [
+            jnp.concatenate(halves(turned[pl.ds(g * C, C), :].T), axis=1) for g in range(groups)
+        ]
+        for slot in range(min(16, planes)):
+            place = jnp.where((((row & (C - 1)) >> 3) == slot) & (source == col), 1.0, 0.0)
+            place = place.astype(jnp.bfloat16)
+            for g in range(groups):
+                p = 16 * g + slot
+                if p < planes:
+                    split[pl.ds(p * C, C), 2 * C : 3 * C] = jnp.dot(
+                        ghosts[g], place, preferred_element_type=jnp.float32
+                    ).astype(jnp.bfloat16)
+
+        lane8 = lanes(8)
+
+        @pl.loop(0, C // 8)
+        def _(r):
+            at = pl.multiple_of(r * 8, 8)
+            east = faces[pl.ds(at, 8), :]
+            for lev in range(2):
+                low_x, high_x, low_y, high_y = [], [], [], []
                 for t in range(2):
-                    for lev in range(2):
-                        j = (k * 2 + t) * 2 + lev
-                        base = (t * 2 + lev) * (C + 8)
-                        south[pl.ds(base, C), :] = fields[0, t, 1, lev]
-                        south[pl.ds(base + C, 8), :] = jnp.broadcast_to(face[j : j + 1], (8, C))
-    faces[...] = faces[...].T
-
-    row = lax.broadcasted_iota(jnp.int32, (2 * C, C), 0)
-    col = lax.broadcasted_iota(jnp.int32, (2 * C, C), 1)
-    source = (row & 7) + 8 * (row // C)
-    ghosts = [
-        jnp.concatenate(halves(turned[pl.ds(g * C, C), :].T), axis=1) for g in range(groups)
-    ]
-    for slot in range(min(16, planes)):
-        place = jnp.where((((row & (C - 1)) >> 3) == slot) & (source == col), 1.0, 0.0)
-        place = place.astype(jnp.bfloat16)
-        for g in range(groups):
-            p = 16 * g + slot
-            if p < planes:
-                split[pl.ds(p * C, C), 2 * C : 3 * C] = jnp.dot(
-                    ghosts[g], place, preferred_element_type=jnp.float32
-                ).astype(jnp.bfloat16)
-
-    lane8 = lanes(8)
+                    j = (k * 2 + t) * 2 + lev
+                    west = fields[0, t, 0, lev, pl.ds(at, 8), :]
+                    low_x.append(west)
+                    high_x.append(
+                        jnp.where(
+                            lane8 == C - 1, pltpu.roll(east, C - 1 - j, 1), pltpu.roll(west, C - 1, 1)
+                        )
+                    )
+                    base = (t * 2 + lev) * (C + 8)
+                    low_y.append(south[pl.ds(base + at, 8), :])
+                    high_y.append(south[pl.ds(base + at + 1, 8), :])
+                along_x = stencil(taps(*low_x), taps(*high_x))
+                along_y = stencil(taps(*low_y), taps(*high_y))
+                centre = 1.0 + along_x[3] + along_y[3]
+                every = [centre] + along_x[:3] + along_x[4:] + along_y[:3] + along_y[4:]
+                for i, value in enumerate(every):
+                    coef[lev * 13 + i, pl.ds(at, 8), :] = value
+
+    rows = min(4, chunk) * C
+
+    @pl.loop(0, chunk * C // rows)
+    def _(b):
+        at = pl.multiple_of(part * (chunk * C) + b * rows, C)
+        moved[pl.ds(pl.multiple_of(b * rows, C), rows), :] = jnp.dot(
+            split[pl.ds(at, rows), :], weights[...], preferred_element_type=jnp.float32
+        )
 
     @pl.loop(0, C // 8)
     def _(r):
         at = pl.multiple_of(r * 8, 8)
-        east = faces[pl.ds(at, 8), :]
         for lev in range(2):
-            low_x, high_x, low_y, high_y = [], [], [], []
-            for t in range(2):
-                j = (k * 2 + t) * 2 + lev
-                west = fields[0, t, 0, lev, pl.ds(at, 8), :]
-                low_x.append(west)
-                high_x.append(
-                    jnp.where(
-                        lane8 == C - 1, pltpu.roll(east, C - 1 - j, 1), pltpu.roll(west, C - 1, 1)
-                    )
-                )
-                base = (t * 2 + lev) * (C + 8)
-                low_y.append(south[pl.ds(base + at, 8), :])
-                high_y.append(south[pl.ds(base + at + 1, 8), :])
-            along_x = stencil(taps(*low_x), taps(*high_x))
-            along_y = stencil(taps(*low_y), taps(*high_y))
-            centre = 1.0 + along_x[3] + along_y[3]
-            every = [centre] + along_x[:3] + along_x[4:] + along_y[:3] + along_y[4:]
-            for i, value in enumerate(every):
-                coef[lev * 13 + i, pl.ds(at, 8), :] = value
-
-    @pl.loop(0, planes // chunk)
-    def _(part):
-        rows = min(4, chunk) * C
-
-        @pl.loop(0, chunk * C // rows)
-        def _(b):
-            at = pl.multiple_of(part * (chunk * C) + b * rows, C)
-            moved[pl.ds(pl.multiple_of(b * rows, C), rows), :] = jnp.dot(
-                split[pl.ds(at, rows), :], weights[...], preferred_element_type=jnp.float32
-            )
-
-        @pl.loop(0, C // 8)
-        def _(r):
-            at = pl.multiple_of(r * 8, 8)
-            for lev in range(2):
-                w = [coef[lev * 13 + i, pl.ds(at, 8), :] for i in range(13)]
-                for s in range(chunk // 2):
-                    p = 2 * s + lev
-                    base = (part * chunk + p) * PAD + 8 + at
-                    here = pl.ds(pl.multiple_of(p * C + at, 8), 8)
-                    total = w[0] * padded[pl.ds(base, 8), :]
-                    for i, d in enumerate(SHIFTS):
-                        total += w[1 + i] * moved[here, i * C : (i + 1) * C]
-                        total += w[7 + i] * padded[pl.ds(base + d, 8), :]
-                    to = pl.multiple_of((part * chunk + p) * C + at, 8)
-                    out[pl.ds(to, 8), :] = total
+            w = [coef[lev * 13 + i, pl.ds(at, 8), :] for i in range(13)]
+            for s in range(chunk // 2):
+                p = 2 * s + lev
+                base = (part * chunk + p) * PAD + 8 + at
+                block = pl.ds(pl.multiple_of(p * C + at, 8), 8)
+                total = w[0] * padded[pl.ds(base, 8), :]
+                for i, d in enumerate(SHIFTS):
+                    total += w[1 + i] * moved[block, i * C : (i + 1) * C]
+                    total += w[7 + i] * padded[pl.ds(base + d, 8), :]
+                out[block, :] = total
 
     if not last:
-        pack_strips(planes, out, strips, turned)
-        fill_slots(near, here, strips, slots)
+        pack_part(planes, chunk, out, 0, part * chunk, strips, turned)
+
+        @pl.when(part == planes // chunk - 1)
+        def _():
+            fill_slots(near, here, strips, slots)
 
 
 def advance(sizes, k, last, near, flips, here, q, fields, got_faces, got):
@@ -515,7 +534,9 @@
     half = sizes["tile"] // 2
     rows = rows_of(planes, 0)
     out_shape = [jax.ShapeDtypeStruct(q.shape, q.dtype)]
-    out_specs = [whole_spec(q.shape)]
+    chunk = chunk_of(planes)
+    moving = pl.BlockSpec((chunk * C, C), lambda i, *_: (i, 0))
+    out_specs = [moving]
     groups = groups_of(planes)
     scratch = [
         pltpu.VMEM((planes * PAD, C), jnp.float32),
@@ -536,9 +557,9 @@
         out_shape=out_shape,
         grid_spec=pltpu.PrefetchScalarGridSpec(
             num_scalar_prefetch=3,
-            grid=(1,),
+            grid=(planes // chunk,),
             in_specs=[
-                whole_spec(q.shape),
+                moving,
                 pl.BlockSpec((1, 2, 2, 2, C, C), lambda i, *_: (k, 0, 0, 0, 0, 0)),
                 whole_spec(got_faces.shape),
                 whole_spec(got.shape),

time: 110 us -> 102 us (0.927); the launches traced: 108 us -> 101 us
  Pallas kernels: 106 us -> 99.3 us
    pallas_call x2, Pallas kernels: 55.7 us -> 51.1 us  [swap_slots(): pl.pallas_call(functools.partial(swap_kernel, sizes), out_shape=jax.Shape...]
    pallas_call x2, Pallas kernels: 41.5 us -> 39.3 us  [advance(): pl.pallas_call(functools.partial(step_kernel, sizes, planes, k, last), ou...]
where the time goes in v4:
time: 102 us; the launch traced here: 101 us
  Pallas kernels  99.3 us (97%)
  local copies, waits for them, and re-layouts  1.3 us (1%)
    pallas_call x2, Pallas kernels, swap_slots(): pl.pallas_call(functools.partial(swap_kernel, sizes), out_shape=jax.Shape...  51.1 us
    pallas_call x2, Pallas kernels, advance(): pl.pallas_call(functools.partial(step_kernel, sizes, planes, k, last), ou...  39.3 us
    pallas_call x1, Pallas kernels, pack_first(): pl.pallas_call(functools.partial(pack_kernel, sizes, planes), out_shape=(...  5.87 us
    pallas_call x1, Pallas kernels, spread_fields(): pl.pallas_call(functools.partial(spread_kernel, sizes), out_shape=(shape,...  3.07 us

profile of v4, /device:TPU:14, one launch (start us, length us, event | category | flops | bytes accessed | tf_op | source)
XLA Modules:
  0.0 101.2 jit_solution(17402424238136780246)
XLA Ops:
  0.0 0.6 pad_add_fusion.here
  0.6 1.3 %copy.7.roots = s32[2,1]{1,0:T(2,128)} copy(s32[2,1]{0,1:T(1,128)} %param.11) | data formatting | bytes 16 | tf_op args[5]
  1.9 3.1 %spread_fields.1 = (f32[2,2,2,2,128,128]{5,4,3,2,1,0:T(8,128)}, f32[2,2,2,2,128,128]{5,4,3,2,1,0:T(8,128)}) custom-call(f32[1,2,2,2,128,128]{5,4,3,2,1,0:T(8,128)} %own_c.1, f32[1,2,2,2,128,128]{5,4,3,2,1,0:T(8,128)} %own_d.1), custom_call_target="tpu_custom_call" | custom-call | tf_op jit(solution)/shard_map/spread_fields/pallas_call | solution.py:172
  5.0 5.9 %pack_first.1 = (f32[8,152,128]{2,1,0:T(8,128)}, f32[4,160,128]{2,1,0:T(8,128)}, f32[2,2,2,2,128,128]{5,4,3,2,1,0:T(8,128)}) custom-call(s32[2,1]{1,0:T(2,128)} %copy.7.roots, s32[1,4]{1,0:T(1,128)} %near.5, s32[2]{0:T(128)} %pad_add_fusion.here, f32[6144,128]{1,0:T(8,128)} %bitcast.4, f32[1,2,2,2,128,128]{5,4,3,2,1,0:T(8,128)} %own_c.1, ...), custom_call_target="tpu_custom_call" | custom-call | tf_op jit(solution)/shard_map/pack_first/pallas_call | solution.py:293
  10.9 26.8 %swap_slots_0.1.got_faces.got = f32[16,152,128]{2,1,0:T(8,128)} custom-call(f32[8,152,128]{2,1,0:T(8,128)} %get-tuple-element.16.slots, f32[4,160,128]{2,1,0:T(8,128)} %get-tuple-element.17.strips), custom_call_target="tpu_custom_call" | custom-call | tf_op jit(solution)/shard_map/swap_slots_0/pallas_call | solution.py:190
  37.6 20.7 %advance_0.1 = (f32[6144,128]{1,0:T(8,128)}, f32[8,144,128]{2,1,0:T(8,128)}, f32[4,152,128]{2,1,0:T(8,128)}) custom-call(s32[1,4]{1,0:T(1,128)} %near.5, s32[1,4]{1,0:T(1,128)} %flips.3, s32[2]{0:T(128)} %pad_add_fusion.here, f32[6144,128]{1,0:T(8,128)} %bitcast.5, f32[2,2,2,2,128,128]{5,4,3,2,1,0:T(8,128)} %get-tuple-element.15.fields, ...), custom_call_target="tpu_custom_call" | custom-call | tf_op jit(solution)/shard_map/advance_0/pallas_call | solution.py:555
  58.4 24.3 %swap_slots_1.1.got = f32[16,144,128]{2,1,0:T(8,128)} custom-call(f32[8,144,128]{2,1,0:T(8,128)} %get-tuple-element.19.slots, f32[4,152,128]{2,1,0:T(8,128)} %get-tuple-element.20.strips), custom_call_target="tpu_custom_call" | custom-call | tf_op jit(solution)/shard_map/swap_slots_1/pallas_call | solution.py:190
  82.7 18.5 %advance_1.1 = f32[6144,128]{1,0:T(8,128)} custom-call(s32[1,4]{1,0:T(1,128)} %near.5, s32[1,4]{1,0:T(1,128)} %flips.3, s32[2]{0:T(128)} %pad_add_fusion.here, f32[6144,128]{1,0:T(8,128)} %get-tuple-element.18.q, f32[2,2,2,2,128,128]{5,4,3,2,1,0:T(8,128)} %get-tuple-element.15.fields, f32[16,152,128]{2,1,0:T(8,128)} %swap_slots_0.1.got_faces.got, ...), custom_call_target="tpu_custom_call" | custom-call | tf_op jit(solution)/shard_map/advance_1/pallas_call | solution.py:555
